TPU v7x, 768 devices: a whole 4x8x12 slice. The times are simulated.
768 devices in a mesh: dp: 24 (over z, core), vocab: 32 (over y, x).
Axes of the slice: x: 4, y: 8, z: 12, core: 2. Of those that a mesh axis runs over, the one named last changes fastest.
Arguments:
- tokens_in: bfloat16 [3072, 8192], P('dp'), may hold values from -80 to 80
- gain: float32 [8192], replicated, may hold values from 0.5 to 1.5
- head_weight: bfloat16 [8192, 16896], P(None, 'vocab'), may hold values from -0.5 to 0.5
- teacher_ids: int32 [3072, 16], P('dp'), may hold values from 0 to 16895
- teacher_weight: float32 [3072, 16], P('dp'), may hold values from 0.05 to 1
- labels: int32 [3072], P('dp'), may hold values from 0 to 16895
Outputs:
- token_loss: float32 [3072], P('dp')
- grad_input: bfloat16 [3072, 8192], P('dp', 'vocab')
- head_grad: float32 [528, 32, 8192], P('dp', 'vocab')
All inputs are finite; a program needn't handle non-finite values.
Results may differ from a plain program's by a relative error of at most 0.015.
Values may be sent and summed in bfloat16 or wider, within the bound.
No kernel may reach another device: no remote copies, remote signals or barrier semaphores. Data moves between devices by JAX's collectives and lax.ppermute only.
A program may use at most 64 MiB of HBM per device.

v0:
```python
import jax
import jax.numpy as jnp
from jax import lax
from jax.sharding import PartitionSpec as P

LABEL_SHARE = 0.5
EPS = 1e-05


def normalize(tokens_in, gain):
    as_float = tokens_in.astype(jnp.float32)
    row_scale = jnp.sqrt(jnp.mean(as_float * as_float, axis=1, keepdims=True) + EPS)
    normed = (as_float / row_scale * gain[None, :]).astype(jnp.bfloat16)
    return (as_float, row_scale, normed)


def targets(teacher_ids, teacher_probs, labels, col_start, col_width):
    columns = col_start + jnp.arange(col_width, dtype=jnp.int32)
    matches = (teacher_ids[:, :, None] == columns[None, None, :]).astype(jnp.float32)
    teacher_part = jnp.sum(teacher_probs[:, :, None] * matches, axis=1)
    label_part = (labels[:, None] == columns[None, :]).astype(jnp.float32)
    return (1.0 - LABEL_SHARE) * teacher_part + LABEL_SHARE * label_part


def head_part(dlogits, normed):
    head_term = lax.dot_general(
        dlogits, normed, (((0,), (0,)), ((), ())), preferred_element_type=jnp.float32
    )
    summed = lax.psum_scatter(
        head_term.astype(jnp.bfloat16), "dp", scatter_dimension=0, tiled=True
    ).astype(jnp.float32)
    return summed[:, None, :]


def input_part(dlogits, head_weight, as_float, row_scale, gain):
    partial_value = lax.dot_general(
        dlogits, head_weight, (((1,), (1,)), ((), ())), preferred_element_type=jnp.float32
    )
    dhidden = lax.psum_scatter(
        partial_value.astype(jnp.bfloat16), "vocab", scatter_dimension=1, tiled=True
    ).astype(jnp.float32)
    feature_count = as_float.shape[1]
    slice_width = dhidden.shape[1]
    slice_start = lax.axis_index("vocab") * slice_width
    local_tokens = lax.dynamic_slice_in_dim(as_float, slice_start, slice_width, 1)
    local_gain = lax.dynamic_slice_in_dim(gain, slice_start, slice_width, 0)
    scaled = dhidden * local_gain[None, :]
    inner_sum = lax.psum(jnp.sum(scaled * local_tokens, axis=1), "vocab")[:, None]
    cubed = row_scale * row_scale * row_scale
    return (scaled / row_scale - local_tokens * inner_sum / (feature_count * cubed)).astype(
        jnp.bfloat16
    )


def local(tokens_in, gain, head_weight, teacher_ids, teacher_weight, labels):
    col_width = head_weight.shape[1]
    col_start = lax.axis_index("vocab") * col_width
    as_float, row_scale, normed = normalize(tokens_in, gain)
    logits = jnp.dot(normed, head_weight, preferred_element_type=jnp.float32)
    teacher_probs = teacher_weight / jnp.sum(teacher_weight, axis=1, keepdims=True)
    target = targets(teacher_ids, teacher_probs, labels, col_start, col_width)
    local_dot = jnp.sum(target * logits, axis=1)
    row_top = lax.pmax(jnp.max(logits, axis=1), "vocab")
    total_exp, total_dot = lax.psum(
        (jnp.sum(jnp.exp(logits - row_top[:, None]), axis=1), local_dot), "vocab"
    )
    lse = row_top + jnp.log(total_exp)
    token_loss = (
        (1.0 - LABEL_SHARE) * jnp.sum(teacher_probs * jnp.log(teacher_probs), axis=1)
        - total_dot
        + lse
    )
    dlogits = (jnp.exp(logits - lse[:, None]) - target).astype(jnp.bfloat16)
    grad_input = input_part(dlogits, head_weight, as_float, row_scale, gain)
    head_grad = head_part(dlogits, normed)
    return (token_loss, grad_input, head_grad)


def solution(mesh):
    in_specs = (P("dp", None), P(), P(None, "vocab"), P("dp", None), P("dp", None), P("dp"))
    out_specs = (P("dp"), P("dp", "vocab"), P("dp", "vocab", None))
    return jax.shard_map(local, mesh=mesh, in_specs=in_specs, out_specs=out_specs, check_vma=False)
```

profile of v0, /device:TPU:64, one launch (start us, length us, event | category | flops | bytes accessed | tf_op | source)
XLA Modules:
  0.0 482.7 jit_solution(5139183552363602148)
XLA Ops:
  7.2 0.0 reduce-scatter.4.cloned.1.call-start
  7.2 2.1 multiply_reduce_fusion
  9.3 0.0 copy-start.1
  9.3 0.0 copy-start.2
  9.3 0.0 copy-start.3
  9.3 6.6 %fusion.5 = (f32[128]{0:T(128)S(1)}, f32[128,528]{0,1:T(8,128)S(1)}) fusion(bf16[8192,528]{0,1:T(8,128)(2,1)} %param.8, f32[8192]{0:T(1024)} %param.7, f32[128]{0:T(128)S(1)} %get-tuple-element.19, bf16[128,8192]{1,0:T(8,128)(2,1)} %param.6), kind=kOutput, calls=%fused_computation.24 | convolution fusion | flops 1111558016 | bytes 11052032 | tf_op jit(solution)/shard_map/dot_general | solution.py:59
  16.0 75.3 %pmax.7 = f32[128]{0:T(128)S(1)} all-reduce(f32[128]{0:T(128)S(1)} %get-tuple-element.20), channel_id=1, replica_groups=mesh['dp'=24,'vocab'=32] {'vocab'}, use_global_device_ids=true, to_apply=%region_7.0 | all-reduce | flops 128 | bytes 1024 | tf_op jit(solution)/shard_map/pmax | solution.py:63
  91.3 0.5 select_reduce_fusion
  91.8 0.2 multiply_reduce_fusion.1
  92.0 69.6 %psum.22 = f32[128]{0:T(128)S(1)} all-reduce(f32[128]{0:T(128)S(1)} %get-tuple-element.13), channel_id=1, replica_groups=mesh['dp'=24,'vocab'=32] {'vocab'}, use_global_device_ids=true, to_apply=%region_9.0 | all-reduce | flops 128 | bytes 1024 | tf_op jit(solution)/shard_map/psum | solution.py:64
  161.6 0.1 subtract_convert_fusion
  161.8 0.0 copy-start
  161.8 0.0 copy-start.4
  161.8 6.8 %convolution_convert_fusion.1 = bf16[128,8192]{1,0:T(8,128)(2,1)} fusion(bf16[128,528]{0,1:T(8,128)(2,1)S(1)} %subtract_convert_fusion, bf16[8192,528]{0,1:T(8,128)(2,1)} %param.8), kind=kOutput, calls=%fused_computation.1 | convolution fusion | flops 1108344832 | bytes 10883072 | tf_op jit(solution)/shard_map/dot_general | solution.py:36
  168.6 0.0 reduce-scatter.4.cloned.1.call-update
  168.7 5.8 %convolution_convert_fusion = bf16[528,8192]{1,0:T(8,128)(2,1)} fusion(bf16[128,528]{0,1:T(8,128)(2,1)S(1)} %subtract_convert_fusion, f32[8192]{0:T(1024)S(1)} %copy-done.4, f32[128]{0:T(128)S(1)} %get-tuple-element.19, bf16[128,8192]{1,0:T(8,128)(2,1)S(1)} %copy-done), kind=kOutput, calls=%fused_computation | convolution fusion | flops 1115815936 | bytes 10916352 | tf_op jit(solution)/shard_map/dot_general | solution.py:26
  174.5 63.0 %fusion = bf16[24,8192]{1,0:T(8,128)(2,1)S(1)} fusion(bf16[528,8192]{1,0:T(8,128)(2,1)} %convolution_convert_fusion), kind=kCustom, calls=%all-reduce-scatter | all-reduce-scatter fusion | flops 4718593 | bytes 9048064
  237.5 1.9 collective-permute-start
  239.4 0.8 slice
  240.3 1.9 collective-permute-start.1
  242.2 2.3 convert_element_type.24
  244.5 0.1 dynamic_slice.6
  244.6 1.3 dynamic-slice.4
  246.5 8.5 %collective-permute-done.1 = bf16[22,8192]{1,0:T(8,128)(2,1)S(1)} collective-permute-done((bf16[22,8192]{1,0:T(8,128)(2,1)}, bf16[22,8192]{1,0:T(8,128)(2,1)S(1)}, u32[]{:S(2)}, u32[]{:S(2)}) %collective-permute-start.1) | collective-permute-done | bytes 360480
  255.0 1.5 concatenate
  256.6 0.1 fusion.1
  256.7 1.6 copy.15
  258.3 142.0 %reduce-scatter.4.cloned.1.call-done = bf16[128,256]{1,0:T(8,128)(2,1)} async-done(((bf16[128,8192]{1,0:T(8,128)(2,1)}), bf16[128,256]{1,0:T(8,128)(2,1)}) %reduce-scatter.4.cloned.1.call-update) | async-done | bytes 65552 | tf_op jit(solution)/shard_map/reduce_scatter | solution.py:39
  400.2 1.0 multiply_reduce_fusion.2
  401.3 72.4 %all-reduce.2 = (f32[128]{0:T(128)S(1)}, f32[128]{0:T(128)S(1)}) all-reduce(f32[128]{0:T(128)S(1)} %get-tuple-element.12, f32[128]{0:T(128)S(1)} %multiply_reduce_fusion.2), channel_id=1, replica_groups=mesh['dp'=24,'vocab'=32] {'vocab'}, use_global_device_ids=true, to_apply=%region_5.0 | all-reduce | flops 256 | bytes 2048 | tf_op jit(solution)/shard_map/psum | solution.py:64
  473.6 0.5 subtract_add_fusion
  474.2 1.7 subtract_convert_fusion.1
  (11 shorter events, 0.1 us)
Async XLA Ops:
  7.2 393.1 %reduce-scatter.4.cloned.1.call-start = ((), (), s32[]{:S(2)}) async-start(), calls=%async_computation.1 | async-start | bytes 2162688 | tf_op jit(solution)/shard_map/reduce_scatter | solution.py:39
  9.3 81.9 %copy-start.1 = (f32[128,16]{0,1:T(8,128)S(1)}, f32[128,16]{0,1:T(8,128)}, u32[]{:S(2)}) copy-start(f32[128,16]{0,1:T(8,128)} %param.10) | copy-start | bytes 24580
  9.3 82.0 %copy-start.2 = (s32[128,16]{0,1:T(8,128)S(1)}, s32[128,16]{0,1:T(8,128)}, u32[]{:S(2)}) copy-start(s32[128,16]{0,1:T(8,128)} %param.9) | copy-start | bytes 24580
  9.3 82.5 %copy-start.3 = (s32[128]{0:T(128)S(1)}, s32[128]{0:T(128)}, u32[]{:S(2)}) copy-start(s32[128]{0:T(128)} %param.11) | copy-start | bytes 1540
  161.8 6.9 %copy-start = (bf16[128,8192]{1,0:T(8,128)(2,1)S(1)}, bf16[128,8192]{1,0:T(8,128)(2,1)}, u32[]{:S(2)}) copy-start(bf16[128,8192]{1,0:T(8,128)(2,1)} %param.6) | copy-start | bytes 6291460
  161.8 6.9 %copy-start.4 = (f32[8192]{0:T(1024)S(1)}, f32[8192]{0:T(1024)}, u32[]{:S(2)}) copy-start(f32[8192]{0:T(1024)} %param.7) | copy-start | bytes 98308
  237.5 17.5 %collective-permute-start = (bf16[24,8192]{1,0:T(8,128)(2,1)S(1)}, bf16[24,8192]{1,0:T(8,128)(2,1)S(1)}, u32[]{:S(2)}, u32[]{:S(2)}) collective-permute-start(bf16[24,8192]{1,0:T(8,128)(2,1)S(1)} %fusion), channel_id=1, source_target_pairs={{0,32},{32,64},{64,96},{96,128},{128,160},{160,192},{192,224},{224... | collective-permute-start | bytes 1179656
  240.3 14.8 %collective-permute-start.1 = (bf16[22,8192]{1,0:T(8,128)(2,1)}, bf16[22,8192]{1,0:T(8,128)(2,1)S(1)}, u32[]{:S(2)}, u32[]{:S(2)}) collective-permute-start(bf16[22,8192]{1,0:T(8,128)(2,1)} %slice), channel_id=1, source_target_pairs={{0,64},{32,96},{64,128},{96,160},{128,192},{160,224},{192,256},{22... | collective-permute-start | bytes 1081352
Sparse Core Ops, SparseCore 0:
  168.8 231.4 reduce-scatter.3
where the time goes:
time: 483 us
  blocking collectives  280 us (58%)
  waiting for transfers between devices  151 us (31%)
  matrix products  19.3 us (4%)
  between operations  14.8 us (3%)
  other arithmetic  8.65 us (2%)
  local copies, waits for them, and re-layouts  5.33 us (1%)
    reduce_scatter x1, waiting for transfers between devices, input_part(): lax.psum_scatter(partial_value.astype(jnp.bfloat16), 'vocab', scatter_dim...  142 us
    psum x2, blocking collectives, local(): lax.psum((jnp.sum(jnp.exp(logits - row_top[:, None]), axis=1), local_dot)...  142 us
    pmax x1, blocking collectives, local(): row_top = lax.pmax(jnp.max(logits, axis=1), 'vocab')  75.3 us
    unnamed x1, blocking collectives  63 us
  transfers between devices with their start and end apart: 3, of which 2 were waited for; matrix products, arithmetic and copies ran while one was open for 16% of the time, Pallas kernels for 0%

commit v1 on v0

v1 whole, which is shorter than its diff:
```python
import jax
import jax.numpy as jnp
from jax import lax
from jax.sharding import Mesh, PartitionSpec as P

LABEL_SHARE = 0.5
EPS = 1e-05
NZ, NC, NY, NX = 12, 2, 8, 4


def normalize(tokens_in, gain):
    as_float = tokens_in.astype(jnp.float32)
    row_scale = jnp.sqrt(jnp.mean(as_float * as_float, axis=1, keepdims=True) + EPS)
    normed = (as_float / row_scale * gain[None, :]).astype(jnp.bfloat16)
    return (row_scale, normed)


def targets(teacher_ids, teacher_probs, labels, col_start, col_width):
    columns = col_start + jnp.arange(col_width, dtype=jnp.int32)
    matches = (teacher_ids[:, :, None] == columns[None, None, :]).astype(jnp.float32)
    teacher_part = jnp.sum(teacher_probs[:, :, None] * matches, axis=1)
    label_part = (labels[:, None] == columns[None, :]).astype(jnp.float32)
    return (1.0 - LABEL_SHARE) * teacher_part + LABEL_SHARE * label_part


def local(tokens_in, gain, head_weight, teacher_ids, teacher_weight, labels):
    tokens, features = tokens_in.shape
    col_width = head_weight.shape[1]
    n_vocab = NY * NX
    block = lax.axis_index("y") * NX + lax.axis_index("x")
    core = lax.axis_index("c")
    swap = [(0, 1), (1, 0)]
    row_scale, normed = normalize(tokens_in, gain)
    other_normed = lax.ppermute(normed, "c", swap)
    logits = jnp.dot(normed, head_weight, preferred_element_type=jnp.float32)
    teacher_probs = teacher_weight / jnp.sum(teacher_weight, axis=1, keepdims=True)
    target = targets(teacher_ids, teacher_probs, labels, block * col_width, col_width)
    top = jnp.max(logits, axis=1)
    exps = jnp.exp(logits - top[:, None])
    stats = jnp.stack(
        [top, jnp.sum(exps, axis=1), jnp.sum(target * logits, axis=1), jnp.sum(exps * logits, axis=1)]
    )
    with jax.named_scope("stats"):
        stats = lax.all_to_all(
            jnp.broadcast_to(stats[None], (n_vocab,) + stats.shape), ("y", "x"), 0, 0
        )
    row_top = jnp.max(stats[:, 0], axis=0)
    weight = jnp.exp(stats[:, 0] - row_top[None])
    total_exp = jnp.sum(weight * stats[:, 1], axis=0)
    total_dot = jnp.sum(stats[:, 2], axis=0)
    mean_logit = jnp.sum(weight * stats[:, 3], axis=0) / total_exp
    lse = row_top + jnp.log(total_exp)
    token_loss = (
        (1.0 - LABEL_SHARE) * jnp.sum(teacher_probs * jnp.log(teacher_probs), axis=1)
        - total_dot
        + lse
    )
    dlogits = (jnp.exp(logits - lse[:, None]) - target).astype(jnp.bfloat16)

    rows = col_width // (NZ * NC)
    by_owner = dlogits.reshape(tokens, NZ, NC, rows)
    mine = lax.dynamic_index_in_dim(by_owner, core, 2, False).reshape(tokens, NZ * rows)
    theirs = lax.dynamic_index_in_dim(by_owner, 1 - core, 2, False).reshape(tokens, NZ * rows)
    other_mine = lax.ppermute(theirs, "c", swap)

    partial_value = lax.dot_general(
        dlogits, head_weight, (((1,), (1,)), ((), ())), preferred_element_type=jnp.float32
    ).astype(jnp.bfloat16)
    width = features // n_vocab
    pieces = partial_value.reshape(tokens, n_vocab, width).transpose(1, 0, 2)
    with jax.named_scope("dhid"):
        pieces = lax.all_to_all(pieces, ("y", "x"), 0, 0)

    head_term = lax.dot_general(
        jnp.concatenate([mine, other_mine], axis=0),
        jnp.concatenate([normed, other_normed], axis=0),
        (((0,), (0,)), ((), ())),
        preferred_element_type=jnp.float32,
    )
    with jax.named_scope("ring"):
        summed = lax.psum_scatter(
            head_term.astype(jnp.bfloat16), "z", scatter_dimension=0, tiled=True
        )
    head_grad = summed.astype(jnp.float32)[:, None, :]

    dhidden = jnp.sum(pieces.astype(jnp.float32), axis=0)
    local_tokens = lax.dynamic_slice_in_dim(tokens_in, block * width, width, 1).astype(jnp.float32)
    local_gain = lax.dynamic_slice_in_dim(gain, block * width, width, 0)
    inner_sum = row_scale * (mean_logit - total_dot)[:, None]
    cubed = row_scale * row_scale * row_scale
    grad_input = (
        dhidden * local_gain[None, :] / row_scale - local_tokens * inner_sum / (features * cubed)
    ).astype(jnp.bfloat16)
    return (token_loss, grad_input, head_grad)


def solution(mesh):
    fine = Mesh(mesh.devices.reshape(NZ, NC, NY, NX), ("z", "c", "y", "x"))
    dp, vocab = ("z", "c"), ("y", "x")
    in_specs = (P(dp, None), P(), P(None, vocab), P(dp, None), P(dp, None), P(dp))
    out_specs = (P(dp), P(dp, vocab), P(dp, vocab, None))
    return jax.shard_map(local, mesh=fine, in_specs=in_specs, out_specs=out_specs, check_vma=False)
```

time: 483 us -> 139 us (0.29)
  blocking collectives: 280 us -> 66.5 us
  waiting for transfers between devices: 151 us -> 17.9 us
  starting transfers between devices: 3.87 us -> 20.5 us
  between operations: 14.8 us -> 1.52 us
    reduce_scatter x1 -> x0, waiting for transfers between devices: 142 us -> none  [input_part(): lax.psum_scatter(partial_value.astype(jnp.bfloat16), 'vocab', scatter_dim...]
    psum x2 -> x0, blocking collectives: 142 us -> none  [local(): lax.psum((jnp.sum(jnp.exp(logits - row_top[:, None]), axis=1), local_dot)...]
    pmax x1 -> x0, blocking collectives: 75.3 us -> none  [local(): row_top = lax.pmax(jnp.max(logits, axis=1), 'vocab')]
    all_to_all x0 -> x2, starting transfers between devices: none -> 14.7 us  [the longest x1 9.95 us: local(): lax.all_to_all(jnp.broadcast_to(stats[None], (n_vocab,) + stats.shape), (...]
    all_to_all x0 -> x2, waiting for transfers between devices: none -> 9.97 us  [the longest x1 9.96 us: local(): lax.all_to_all(jnp.broadcast_to(stats[None], (n_vocab,) + stats.shape), (...]
  transfers between devices with their start and end apart: 3 -> 5, of which waited for: 2 -> 2; matrix products, arithmetic and copies ran while one was open for 16% -> 66% of each run, Pallas kernels for 0% -> 0%
where the time goes in v1:
time: 139 us
  blocking collectives  66.5 us (48%)
  starting transfers between devices  20.5 us (15%)
  waiting for transfers between devices  17.9 us (13%)
  matrix products  16.1 us (12%)
  other arithmetic  9.31 us (7%)
  local copies, waits for them, and re-layouts  6.99 us (5%)
  between operations  1.52 us (1%)
    unnamed x1, blocking collectives  66.5 us
    all_to_all x1, waiting for transfers between devices, local(): lax.all_to_all(jnp.broadcast_to(stats[None], (n_vocab,) + stats.shape), (...  9.96 us
    all_to_all x1, starting transfers between devices, local(): lax.all_to_all(jnp.broadcast_to(stats[None], (n_vocab,) + stats.shape), (...  9.95 us
    unnamed x1, waiting for transfers between devices  7.93 us
    dot_general x1, matrix products, local(): logits = jnp.dot(normed, head_weight, preferred_element_type=jnp.float32)  5.88 us
    dot_general x1, matrix products, local(): lax.dot_general(dlogits, head_weight, (((1,), (1,)), ((), ())), preferred...  5.31 us
    dot_general x1, matrix products, local(): lax.dot_general(jnp.concatenate([mine, other_mine], axis=0), jnp.concaten...  4.88 us
    all_to_all x1, starting transfers between devices, local(): pieces = lax.all_to_all(pieces, ('y', 'x'), 0, 0)  4.76 us
  transfers between devices with their start and end apart: 5, of which 2 were waited for; matrix products, arithmetic and copies ran while one was open for 66% of the time, Pallas kernels for 0%

profile of v1, /device:TPU:64, one launch (start us, length us, event | category | flops | bytes accessed | tf_op | source)
XLA Modules:
  0.0 138.8 jit_solution(8985135724617402896)
XLA Ops:
  0.6 2.1 %fusion.1 = f32[128]{0:T(128)S(1)} fusion(bf16[128,8192]{1,0:T(8,128)(2,1)} %param.6), kind=kLoop, calls=%fused_computation.5 | loop fusion | flops 3145600 | bytes 2097664 | tf_op jit(solution)/shard_map/reduce_sum | solution.py:13
  2.7 2.2 %fusion.3 = bf16[128,8192]{1,0:T(8,128)(2,1)S(1)} fusion(bf16[128,8192]{1,0:T(8,128)(2,1)} %param.6, f32[8192]{0:T(1024)} %param.7, f32[128]{0:T(128)S(1)} %get-tuple-element.35), kind=kLoop, calls=%fused_computation.7 | loop fusion | flops 4194304 | bytes 4227584 | tf_op jit(solution)/shard_map/convert_element_type | solution.py:14
  4.9 1.9 %collective-permute-start.1 = (bf16[128,8192]{1,0:T(8,128)(2,1)S(1)}, bf16[128,8192]{1,0:T(8,128)(2,1)}, u32[]{:S(2)}, u32[]{:S(2)}) collective-permute-start(bf16[128,8192]{1,0:T(8,128)(2,1)S(1)} %fusion.3), channel_id=1, source_target_pairs={{0,32},{32,0},{1,33},{33,1},{2,34},{34,2},{3,35},{35,3},{4,36},{36... | collective-permute-start | bytes 6291464 | tf_op jit(solution)/shard_map/ppermute | solution.py:34
  6.9 0.0 copy-start
  6.9 0.0 copy-start.1
  6.9 0.0 copy-start.2
  6.9 5.9 %fusion.16 = (f32[128]{0:T(128)S(1)}, f32[128,528]{0,1:T(8,128)S(1)}) fusion(bf16[128,8192]{1,0:T(8,128)(2,1)S(1)} %fusion.3, bf16[8192,528]{0,1:T(8,128)(2,1)} %param.8), kind=kOutput, calls=%fused_computation.43 | convolution fusion | flops 1107363712 | bytes 11018752 | tf_op jit(solution)/shard_map/dot_general | solution.py:35
  12.9 0.5 select_reduce_fusion
  13.4 0.2 fusion.8
  13.5 0.6 broadcast_in_dim.7
  14.2 9.9 %all-to-all-start = ((f32[32,4,128]{2,1,0:T(4,128)}), f32[32,4,128]{2,1,0:T(4,128)S(1)}, u32[]{:S(2)}, u32[]{:S(2)}) async-start(f32[32,4,128]{2,1,0:T(4,128)} %broadcast_in_dim.7), calls=%async_computation | async-start | bytes 131072 | tf_op jit(solution)/shard_map/stats/all_to_all | solution.py:44
  24.1 10.0 %all-to-all-done = f32[32,4,128]{2,1,0:T(4,128)S(1)} async-done(((f32[32,4,128]{2,1,0:T(4,128)}), f32[32,4,128]{2,1,0:T(4,128)S(1)}, u32[]{:S(2)}, u32[]{:S(2)}) %all-to-all-start) | async-done | bytes 65568 | tf_op jit(solution)/shard_map/stats/all_to_all | solution.py:44
  34.2 0.5 subtract_add_fusion
  34.7 0.1 subtract_convert_fusion
  35.0 1.9 %collective-permute-start = (bf16[128,264]{0,1:T(8,128)(2,1)S(1)}, bf16[128,264]{0,1:T(8,128)(2,1)S(1)}, u32[]{:S(2)}, u32[]{:S(2)}) collective-permute-start(bf16[128,264]{0,1:T(8,128)(2,1)S(1)} %reshape.74), channel_id=1, source_target_pairs={{0,32},{32,0},{1,33},{33,1},{2,34},{34,2},{3,35},{35,3},{4,36},{36... | collective-permute-start | bytes 202760 | tf_op jit(solution)/shard_map/ppermute | solution.py:64
  36.9 5.3 %convolution_convert_fusion.1 = bf16[128,8192]{1,0:T(8,128)(2,1)S(1)} fusion(bf16[128,528]{0,1:T(8,128)(2,1)S(1)} %subtract_convert_fusion, bf16[8192,528]{0,1:T(8,128)(2,1)} %param.8), kind=kOutput, calls=%fused_computation.1 | convolution fusion | flops 1108344832 | bytes 10883072 | tf_op jit(solution)/shard_map/dot_general | solution.py:66
  42.3 1.6 %copy.36 = bf16[16,32,8,256]{3,2,0,1:T(8,128)(2,1)} copy(bf16[16,32,8,256]{3,2,1,0:T(8,128)(2,1)S(1)} %bitcast.37) | data formatting | bytes 4194304 | tf_op jit(solution)/shard_map/reshape | solution.py:70
  43.9 4.8 %all-to-all-start.1 = ((bf16[32,128,256]{2,1,0:T(8,128)(2,1)}), bf16[32,128,256]{2,1,0:T(8,128)(2,1)}, u32[]{:S(2)}, u32[]{:S(2)}) async-start(bf16[32,128,256]{2,1,0:T(8,128)(2,1)} %bitcast.38), calls=%async_computation.1 | async-start | bytes 4194304 | tf_op jit(solution)/shard_map/dhid/all_to_all | solution.py:72
  48.7 0.0 collective-permute-done
  48.7 4.9 %convolution_convert_fusion = bf16[264,8192]{1,0:T(8,128)(2,1)} fusion(bf16[128,8192]{1,0:T(8,128)(2,1)} %collective-permute-done.1, bf16[128,8192]{1,0:T(8,128)(2,1)S(1)} %fusion.3, bf16[128,264]{0,1:T(8,128)(2,1)S(1)} %collective-permute-done, bf16[128,264]{0,1:T(8,128)(2,1)S(1)} %reshape.73), kind=kOutput, calls=%fused_computation | convolution fusion | flops 1118117888 | bytes 8654848 | tf_op jit(solution)/shard_map/dot_general | solution.py:74
  53.6 66.5 %fusion = bf16[24,8192]{1,0:T(8,128)(2,1)S(1)} fusion(bf16[264,8192]{1,0:T(8,128)(2,1)} %convolution_convert_fusion), kind=kCustom, calls=%all-reduce-scatter | all-reduce-scatter fusion | flops 2359297 | bytes 4722688
  120.1 0.1 slice.21
  120.2 1.9 %collective-permute-start.2 = (bf16[22,8192]{1,0:T(8,128)(2,1)S(1)}, bf16[22,8192]{1,0:T(8,128)(2,1)S(1)}, u32[]{:S(2)}, u32[]{:S(2)}) collective-permute-start(bf16[22,8192]{1,0:T(8,128)(2,1)S(1)} %slice.21), channel_id=1, source_target_pairs={{0,64},{64,128},{128,192},{192,256},{256,320},{320,384},{384,448},... | collective-permute-start | bytes 1081352
  122.1 0.8 dynamic_slice.13
  122.9 1.3 dynamic-slice.4
  124.8 7.9 %collective-permute-done.2 = bf16[22,8192]{1,0:T(8,128)(2,1)S(1)} collective-permute-done((bf16[22,8192]{1,0:T(8,128)(2,1)S(1)}, bf16[22,8192]{1,0:T(8,128)(2,1)S(1)}, u32[]{:S(2)}, u32[]{:S(2)}) %collective-permute-start.2) | collective-permute-done | bytes 360480
  132.8 0.8 concatenate.8
  133.6 0.1 fusion.7
  133.7 1.6 %copy.31 = f32[22,1,8192]{2,1,0:T(1,128)} copy(f32[22,1,8192]{2,0,1:T(8,128)S(1)} %fusion.7) | data formatting | bytes 1441792
  135.3 0.0 all-to-all-done.1
  135.3 1.9 %convert_reduce_fusion = f32[128,256]{1,0:T(8,128)S(1)} fusion(bf16[32,128,256]{2,1,0:T(8,128)(2,1)} %all-to-all-done.1), kind=kLoop, calls=%fused_computation.11 | loop fusion | flops 2064384 | bytes 2228224 | tf_op jit(solution)/shard_map/reduce_sum | solution.py:86
  137.2 1.6 %subtract_convert_fusion.1 = bf16[128,256]{1,0:T(8,128)(2,1)} fusion(f32[128,256]{1,0:T(8,128)S(1)} %convert_reduce_fusion, f32[128]{0:T(128)S(1)} %get-tuple-element.34, f32[128]{0:T(128)S(1)} %get-tuple-element.33, bf16[128,8192]{1,0:T(8,128)(2,1)} %param.6, s32[]{:T(128)S(6)} %select_n.11, f32[128]{0:T(128)S(1)} %get-tuple-element.35, ...), kind=kLoop, calls=%fused_computation.24 | loop fusion | flops 229376 | bytes 264708 | tf_op jit(solution)/shard_map/convert_element_type | solution.py:93
  (17 shorter events, 0.3 us)
Async XLA Ops:
  4.9 43.8 %collective-permute-start.1 = (bf16[128,8192]{1,0:T(8,128)(2,1)S(1)}, bf16[128,8192]{1,0:T(8,128)(2,1)}, u32[]{:S(2)}, u32[]{:S(2)}) collective-permute-start(bf16[128,8192]{1,0:T(8,128)(2,1)S(1)} %fusion.3), channel_id=1, source_target_pairs={{0,32},{32,0},{1,33},{33,1},{2,34},{34,2},{3,35},{35,3},{4,36},{36... | collective-permute-start | bytes 6291464 | tf_op jit(solution)/shard_map/ppermute | solution.py:34
  6.9 5.9 %copy-start = (f32[128,16]{0,1:T(8,128)S(1)}, f32[128,16]{0,1:T(8,128)}, u32[]{:S(2)}) copy-start(f32[128,16]{0,1:T(8,128)} %param.10) | copy-start | bytes 24580
  6.9 6.0 %copy-start.1 = (s32[128,16]{0,1:T(8,128)S(1)}, s32[128,16]{0,1:T(8,128)}, u32[]{:S(2)}) copy-start(s32[128,16]{0,1:T(8,128)} %param.9) | copy-start | bytes 24580
  6.9 6.5 %copy-start.2 = (s32[128]{0:T(128)S(1)}, s32[128]{0:T(128)}, u32[]{:S(2)}) copy-start(s32[128]{0:T(128)} %param.11) | copy-start | bytes 1540
  14.2 19.9 %all-to-all-start = ((f32[32,4,128]{2,1,0:T(4,128)}), f32[32,4,128]{2,1,0:T(4,128)S(1)}, u32[]{:S(2)}, u32[]{:S(2)}) async-start(f32[32,4,128]{2,1,0:T(4,128)} %broadcast_in_dim.7), calls=%async_computation | async-start | bytes 131072 | tf_op jit(solution)/shard_map/stats/all_to_all | solution.py:44
  35.0 13.7 %collective-permute-start = (bf16[128,264]{0,1:T(8,128)(2,1)S(1)}, bf16[128,264]{0,1:T(8,128)(2,1)S(1)}, u32[]{:S(2)}, u32[]{:S(2)}) collective-permute-start(bf16[128,264]{0,1:T(8,128)(2,1)S(1)} %reshape.74), channel_id=1, source_target_pairs={{0,32},{32,0},{1,33},{33,1},{2,34},{34,2},{3,35},{35,3},{4,36},{36... | collective-permute-start | bytes 202760 | tf_op jit(solution)/shard_map/ppermute | solution.py:64
  43.9 91.4 %all-to-all-start.1 = ((bf16[32,128,256]{2,1,0:T(8,128)(2,1)}), bf16[32,128,256]{2,1,0:T(8,128)(2,1)}, u32[]{:S(2)}, u32[]{:S(2)}) async-start(bf16[32,128,256]{2,1,0:T(8,128)(2,1)} %bitcast.38), calls=%async_computation.1 | async-start | bytes 4194304 | tf_op jit(solution)/shard_map/dhid/all_to_all | solution.py:72
  120.2 12.5 %collective-permute-start.2 = (bf16[22,8192]{1,0:T(8,128)(2,1)S(1)}, bf16[22,8192]{1,0:T(8,128)(2,1)S(1)}, u32[]{:S(2)}, u32[]{:S(2)}) collective-permute-start(bf16[22,8192]{1,0:T(8,128)(2,1)S(1)} %slice.21), channel_id=1, source_target_pairs={{0,64},{64,128},{128,192},{192,256},{256,320},{320,384},{384,448},... | collective-permute-start | bytes 1081352

commit v2 on v1

--- a/solution.py
+++ b/solution.py
@@ -2,6 +2,7 @@
 import jax.numpy as jnp
 from jax import lax
 from jax.sharding import Mesh, PartitionSpec as P
+
 
 LABEL_SHARE = 0.5
 EPS = 1e-05
@@ -40,10 +41,9 @@
     stats = jnp.stack(
         [top, jnp.sum(exps, axis=1), jnp.sum(target * logits, axis=1), jnp.sum(exps * logits, axis=1)]
     )
-    with jax.named_scope("stats"):
-        stats = lax.all_to_all(
-            jnp.broadcast_to(stats[None], (n_vocab,) + stats.shape), ("y", "x"), 0, 0
-        )
+    stats = lax.all_to_all(
+        jnp.broadcast_to(stats[None], (n_vocab,) + stats.shape), ("y", "x"), 0, 0
+    )
     row_top = jnp.max(stats[:, 0], axis=0)
     weight = jnp.exp(stats[:, 0] - row_top[None])
     total_exp = jnp.sum(weight * stats[:, 1], axis=0)
@@ -58,9 +58,9 @@
     dlogits = (jnp.exp(logits - lse[:, None]) - target).astype(jnp.bfloat16)
 
     rows = col_width // (NZ * NC)
-    by_owner = dlogits.reshape(tokens, NZ, NC, rows)
-    mine = lax.dynamic_index_in_dim(by_owner, core, 2, False).reshape(tokens, NZ * rows)
-    theirs = lax.dynamic_index_in_dim(by_owner, 1 - core, 2, False).reshape(tokens, NZ * rows)
+    by_owner = jnp.pad(dlogits.reshape(tokens, NZ, NC, rows), ((0, 0), (0, 0), (0, 0), (0, 2)))
+    mine = lax.dynamic_index_in_dim(by_owner, core, 2, False).reshape(tokens, -1)
+    theirs = lax.dynamic_index_in_dim(by_owner, 1 - core, 2, False).reshape(tokens, -1)
     other_mine = lax.ppermute(theirs, "c", swap)
 
     partial_value = lax.dot_general(
@@ -68,8 +68,7 @@
     ).astype(jnp.bfloat16)
     width = features // n_vocab
     pieces = partial_value.reshape(tokens, n_vocab, width).transpose(1, 0, 2)
-    with jax.named_scope("dhid"):
-        pieces = lax.all_to_all(pieces, ("y", "x"), 0, 0)
+    pieces = lax.all_to_all(pieces, ("y", "x"), 0, 0)
 
     head_term = lax.dot_general(
         jnp.concatenate([mine, other_mine], axis=0),
@@ -77,11 +76,8 @@
         (((0,), (0,)), ((), ())),
         preferred_element_type=jnp.float32,
     )
-    with jax.named_scope("ring"):
-        summed = lax.psum_scatter(
-            head_term.astype(jnp.bfloat16), "z", scatter_dimension=0, tiled=True
-        )
-    head_grad = summed.astype(jnp.float32)[:, None, :]
+    summed = lax.psum_scatter(head_term.astype(jnp.bfloat16), "z", scatter_dimension=0, tiled=True)
+    head_grad = summed[:rows].astype(jnp.float32)[:, None, :]
 
     dhidden = jnp.sum(pieces.astype(jnp.float32), axis=0)
     local_tokens = lax.dynamic_slice_in_dim(tokens_in, block * width, width, 1).astype(jnp.float32)

time: 139 us -> 132 us (0.950)
  the two profiles are of different devices: /device:TPU:64 before, /device:TPU:4 now
where the time goes in v2:
time: 132 us; the launch traced here: 131 us
  waiting for transfers between devices  64.4 us (49%)
  starting transfers between devices  22.8 us (17%)
  matrix products  16.3 us (12%)
  between operations  14.2 us (11%)
  other arithmetic  8.68 us (7%)
  local copies, waits for them, and re-layouts  4.77 us (4%)
    all_to_all x1, waiting for transfers between devices, local(): pieces = lax.all_to_all(pieces, ('y', 'x'), 0, 0)  49.2 us
    all_to_all x1, starting transfers between devices, local(): lax.all_to_all(jnp.broadcast_to(stats[None], (n_vocab,) + stats.shape), (...  13 us
    all_to_all x1, waiting for transfers between devices, local(): lax.all_to_all(jnp.broadcast_to(stats[None], (n_vocab,) + stats.shape), (...  8.28 us
    all_to_all x1, starting transfers between devices, local(): pieces = lax.all_to_all(pieces, ('y', 'x'), 0, 0)  5.94 us
    dot_general x1, matrix products, local(): logits = jnp.dot(normed, head_weight, preferred_element_type=jnp.float32)  5.88 us
    reduce_scatter x1, waiting for transfers between devices, local(): lax.psum_scatter(head_term.astype(jnp.bfloat16), 'z', scatter_dimension=0...  5.67 us
    dot_general x1, matrix products, local(): lax.dot_general(dlogits, head_weight, (((1,), (1,)), ((), ())), preferred...  5.31 us
    dot_general x1, matrix products, local(): lax.dot_general(jnp.concatenate([mine, other_mine], axis=0), jnp.concaten...  5.12 us
  transfers between devices with their start and end apart: 5, of which 4 were waited for; matrix products, arithmetic and copies ran while one was open for 13% of the time, Pallas kernels for 0%

profile of v2, /device:TPU:4, one launch (start us, length us, event | category | flops | bytes accessed | tf_op | source)
XLA Modules:
  0.0 131.1 jit_solution(363267314444331560)
XLA Ops:
  7.2 0.0 copy-start
  7.2 0.0 copy-start.1
  7.2 2.1 %fusion = f32[128]{0:T(128)S(1)} fusion(bf16[128,8192]{1,0:T(8,128)(2,1)} %param.6), kind=kLoop, calls=%fused_computation.5 | loop fusion | flops 3145600 | bytes 2097664 | tf_op jit(solution)/shard_map/reduce_sum | solution.py:14
  9.3 2.2 %fusion.2 = bf16[128,8192]{1,0:T(8,128)(2,1)S(1)} fusion(bf16[128,8192]{1,0:T(8,128)(2,1)} %param.6, f32[8192]{0:T(1024)} %param.7, f32[128]{0:T(128)S(1)} %get-tuple-element.35), kind=kLoop, calls=%fused_computation.7 | loop fusion | flops 4194304 | bytes 4227584 | tf_op jit(solution)/shard_map/convert_element_type | solution.py:15
  11.5 1.9 %collective-permute-start.1 = (bf16[128,8192]{1,0:T(8,128)(2,1)S(1)}, bf16[128,8192]{1,0:T(8,128)(2,1)}, u32[]{:S(2)}, u32[]{:S(2)}) collective-permute-start(bf16[128,8192]{1,0:T(8,128)(2,1)S(1)} %fusion.2), channel_id=1, source_target_pairs={{0,32},{32,0},{1,33},{33,1},{2,34},{34,2},{3,35},{35,3},{4,36},{36... | collective-permute-start | bytes 6291464 | tf_op jit(solution)/shard_map/ppermute | solution.py:35
  13.4 0.0 copy-done
  13.5 0.0 copy-done.1
  13.5 0.5 select_reduce_fusion
  14.0 0.0 copy-start.2
  14.0 5.9 %fusion.15 = (f32[128]{0:T(128)S(1)}, f32[128,528]{0,1:T(8,128)S(1)}) fusion(bf16[128,8192]{1,0:T(8,128)(2,1)S(1)} %fusion.2, bf16[8192,528]{0,1:T(8,128)(2,1)} %param.8), kind=kOutput, calls=%fused_computation.43 | convolution fusion | flops 1107363712 | bytes 11018752 | tf_op jit(solution)/shard_map/dot_general | solution.py:36
  19.9 0.2 fusion.7
  20.1 0.6 broadcast_in_dim.7
  20.7 13.0 %all-to-all-start = ((f32[32,4,128]{2,1,0:T(4,128)}), f32[32,4,128]{2,1,0:T(4,128)S(1)}, u32[]{:S(2)}, u32[]{:S(2)}) async-start(f32[32,4,128]{2,1,0:T(4,128)} %broadcast_in_dim.7), calls=%async_computation | async-start | bytes 131072 | tf_op jit(solution)/shard_map/all_to_all | solution.py:44
  33.7 0.0 reduce-scatter.2.cloned.1.call-start
  33.8 8.3 %all-to-all-done = f32[32,4,128]{2,1,0:T(4,128)S(1)} async-done(((f32[32,4,128]{2,1,0:T(4,128)}), f32[32,4,128]{2,1,0:T(4,128)S(1)}, u32[]{:S(2)}, u32[]{:S(2)}) %all-to-all-start) | async-done | bytes 65568 | tf_op jit(solution)/shard_map/all_to_all | solution.py:44
  42.2 0.5 subtract_add_fusion
  42.7 0.1 subtract_convert_fusion
  42.9 1.9 %collective-permute-start = (bf16[128,288]{0,1:T(8,128)(2,1)S(1)}, bf16[128,288]{0,1:T(8,128)(2,1)S(1)}, u32[]{:S(2)}, u32[]{:S(2)}) collective-permute-start(bf16[128,288]{0,1:T(8,128)(2,1)S(1)} %bitcast.37), channel_id=1, source_target_pairs={{0,32},{32,0},{1,33},{33,1},{2,34},{34,2},{3,35},{35,3},{4,36},{36... | collective-permute-start | bytes 221192 | tf_op jit(solution)/shard_map/ppermute | solution.py:64
  44.9 1.2 collective-permute-done
  46.1 0.0 collective-permute-done.1
  46.1 5.1 %convolution_convert_fusion = bf16[288,8192]{1,0:T(8,128)(2,1)} fusion(bf16[128,8192]{1,0:T(8,128)(2,1)} %collective-permute-done.1, bf16[128,8192]{1,0:T(8,128)(2,1)S(1)} %fusion.2, bf16[128,288]{0,1:T(8,128)(2,1)S(1)} %collective-permute-done, bf16[128,288]{0,1:T(8,128)(2,1)S(1)} %bitcast.36), kind=kOutput, calls=%fused_computation | convolution fusion | flops 1219002368 | bytes 9060352 | tf_op jit(solution)/shard_map/dot_general | solution.py:73
  51.2 0.0 reduce-scatter.2.cloned.1.call-update
  51.2 5.3 %convolution_convert_fusion.1 = bf16[128,8192]{1,0:T(8,128)(2,1)S(1)} fusion(bf16[128,528]{0,1:T(8,128)(2,1)S(1)} %subtract_convert_fusion, bf16[8192,528]{0,1:T(8,128)(2,1)} %param.8), kind=kOutput, calls=%fused_computation.1 | convolution fusion | flops 1108344832 | bytes 10883072 | tf_op jit(solution)/shard_map/dot_general | solution.py:66
  56.5 1.6 %copy.36 = bf16[16,32,8,256]{3,2,0,1:T(8,128)(2,1)} copy(bf16[16,32,8,256]{3,2,1,0:T(8,128)(2,1)S(1)} %bitcast.32) | data formatting | bytes 4194304 | tf_op jit(solution)/shard_map/reshape | solution.py:70
  58.2 5.9 %all-to-all-start.1 = ((bf16[32,128,256]{2,1,0:T(8,128)(2,1)}), bf16[32,128,256]{2,1,0:T(8,128)(2,1)S(1)}, u32[]{:S(2)}, u32[]{:S(2)}) async-start(bf16[32,128,256]{2,1,0:T(8,128)(2,1)} %bitcast.33), calls=%async_computation.1 | async-start | bytes 4194304 | tf_op jit(solution)/shard_map/all_to_all | solution.py:71
  64.1 0.8 dynamic_slice.13
  64.9 49.2 %all-to-all-done.1 = bf16[32,128,256]{2,1,0:T(8,128)(2,1)S(1)} async-done(((bf16[32,128,256]{2,1,0:T(8,128)(2,1)}), bf16[32,128,256]{2,1,0:T(8,128)(2,1)S(1)}, u32[]{:S(2)}, u32[]{:S(2)}) %all-to-all-start.1) | async-done | bytes 2097184 | tf_op jit(solution)/shard_map/all_to_all | solution.py:71
  114.1 0.3 convert_reduce_fusion
  114.4 1.6 %subtract_convert_fusion.1 = bf16[128,256]{1,0:T(8,128)(2,1)} fusion(f32[128,256]{1,0:T(8,128)S(1)} %convert_reduce_fusion, f32[128]{0:T(128)S(1)} %get-tuple-element.34, f32[128]{0:T(128)S(1)} %get-tuple-element.33, bf16[128,8192]{1,0:T(8,128)(2,1)} %param.6, s32[]{:T(128)S(6)} %select_n.11, f32[128]{0:T(128)S(1)} %get-tuple-element.35, ...), kind=kLoop, calls=%fused_computation.24 | loop fusion | flops 229376 | bytes 264708 | tf_op jit(solution)/shard_map/convert_element_type | solution.py:89
  116.0 5.7 %reduce-scatter.2.cloned.1.call-done = bf16[24,8192]{1,0:T(8,128)(2,1)} async-done(((bf16[288,8192]{1,0:T(8,128)(2,1)}), bf16[24,8192]{1,0:T(8,128)(2,1)}) %reduce-scatter.2.cloned.1.call-update) | async-done | bytes 393232 | tf_op jit(solution)/shard_map/reduce_scatter | solution.py:79
  121.6 1.0 fusion.6
  122.7 1.6 %copy.31 = f32[22,1,8192]{2,1,0:T(1,128)} copy(f32[22,1,8192]{2,0,1:T(8,128)S(1)} %fusion.6) | data formatting | bytes 1441792
  (12 shorter events, 0.3 us)
Async XLA Ops:
  7.2 6.3 %copy-start = (f32[128,16]{0,1:T(8,128)S(1)}, f32[128,16]{0,1:T(8,128)}, u32[]{:S(2)}) copy-start(f32[128,16]{0,1:T(8,128)} %param.10) | copy-start | bytes 24580
  7.2 6.3 %copy-start.1 = (s32[128,16]{0,1:T(8,128)S(1)}, s32[128,16]{0,1:T(8,128)}, u32[]{:S(2)}) copy-start(s32[128,16]{0,1:T(8,128)} %param.9) | copy-start | bytes 24580
  11.5 34.6 %collective-permute-start.1 = (bf16[128,8192]{1,0:T(8,128)(2,1)S(1)}, bf16[128,8192]{1,0:T(8,128)(2,1)}, u32[]{:S(2)}, u32[]{:S(2)}) collective-permute-start(bf16[128,8192]{1,0:T(8,128)(2,1)S(1)} %fusion.2), channel_id=1, source_target_pairs={{0,32},{32,0},{1,33},{33,1},{2,34},{34,2},{3,35},{35,3},{4,36},{36... | collective-permute-start | bytes 6291464 | tf_op jit(solution)/shard_map/ppermute | solution.py:35
  14.0 5.9 %copy-start.2 = (s32[128]{0:T(128)S(1)}, s32[128]{0:T(128)}, u32[]{:S(2)}) copy-start(s32[128]{0:T(128)} %param.11) | copy-start | bytes 1540
  20.7 21.3 %all-to-all-start = ((f32[32,4,128]{2,1,0:T(4,128)}), f32[32,4,128]{2,1,0:T(4,128)S(1)}, u32[]{:S(2)}, u32[]{:S(2)}) async-start(f32[32,4,128]{2,1,0:T(4,128)} %broadcast_in_dim.7), calls=%async_computation | async-start | bytes 131072 | tf_op jit(solution)/shard_map/all_to_all | solution.py:44
  33.7 87.9 %reduce-scatter.2.cloned.1.call-start = ((), (), s32[]{:S(2)}) async-start(), calls=%async_computation.3 | async-start | bytes 5111808 | tf_op jit(solution)/shard_map/reduce_scatter | solution.py:79
  42.9 3.2 %collective-permute-start = (bf16[128,288]{0,1:T(8,128)(2,1)S(1)}, bf16[128,288]{0,1:T(8,128)(2,1)S(1)}, u32[]{:S(2)}, u32[]{:S(2)}) collective-permute-start(bf16[128,288]{0,1:T(8,128)(2,1)S(1)} %bitcast.37), channel_id=1, source_target_pairs={{0,32},{32,0},{1,33},{33,1},{2,34},{34,2},{3,35},{35,3},{4,36},{36... | collective-permute-start | bytes 221192 | tf_op jit(solution)/shard_map/ppermute | solution.py:64
  58.2 55.9 %all-to-all-start.1 = ((bf16[32,128,256]{2,1,0:T(8,128)(2,1)}), bf16[32,128,256]{2,1,0:T(8,128)(2,1)S(1)}, u32[]{:S(2)}, u32[]{:S(2)}) async-start(bf16[32,128,256]{2,1,0:T(8,128)(2,1)} %bitcast.33), calls=%async_computation.1 | async-start | bytes 4194304 | tf_op jit(solution)/shard_map/all_to_all | solution.py:71
Sparse Core Ops, SparseCore 0:
  51.3 70.2 reduce-scatter.1

commit v3 on v2

v3 whole, which is shorter than its diff:
```python
import jax
import jax.numpy as jnp
from jax import lax
from jax.experimental import pallas as pl
from jax.experimental.pallas import tpu as pltpu
from jax.sharding import Mesh, PartitionSpec as P


LABEL_SHARE = 0.5
EPS = 1e-05
NZ, NC, NY, NX = 12, 2, 8, 4


def front_kernel(
    start_ref, x_hbm, gain_ref, w_hbm, ids_ref, weight_ref, label_ref,
    normed_hbm, scale_ref, logits_ref, target_ref, stats_ref,
    x_buf, w_buf, normed_buf, x_sem, w_sem, out_sem,
):
    tokens, features = x_buf.shape
    cols = w_buf.shape[0]
    parts = w_sem.shape[0]
    rows = cols // parts
    step = 1024
    copy_x = pltpu.make_async_copy(x_hbm, x_buf, x_sem)
    copy_x.start()
    copies = []
    for p in range(parts):
        part = pl.ds(p * rows, rows)
        copies.append(pltpu.make_async_copy(w_hbm.at[part], w_buf.at[part], w_sem.at[p]))
        copies[-1].start()

    probs = weight_ref[...] / jnp.sum(weight_ref[...], axis=0, keepdims=True)
    columns = start_ref[0] + lax.broadcasted_iota(jnp.int32, (cols, tokens), 0)
    teacher_part = jnp.zeros((cols, tokens), jnp.float32)
    for k in range(ids_ref.shape[0]):
        teacher_part += jnp.where(ids_ref[k : k + 1, :] == columns, probs[k : k + 1, :], 0.0)
    label_part = jnp.where(label_ref[...] == columns, LABEL_SHARE, 0.0)
    target_ref[...] = (1.0 - LABEL_SHARE) * teacher_part + label_part

    copy_x.wait()
    total = jnp.zeros((tokens, 128), jnp.float32)
    for f in range(0, features, step):
        chunk = x_buf[:, f : f + step].astype(jnp.float32)
        chunk = chunk * chunk
        for g in range(0, step, 128):
            total += chunk[:, g : g + 128]
    scale = jnp.sqrt(jnp.sum(total, axis=1, keepdims=True) / features + EPS)
    scale_ref[...] = scale
    inverse = 1.0 / scale
    for f in range(0, features, step):
        chunk = x_buf[:, f : f + step].astype(jnp.float32)
        normed_buf[:, f : f + step] = (chunk * inverse * gain_ref[:, f : f + step]).astype(
            jnp.bfloat16
        )
    copy_out = pltpu.make_async_copy(normed_buf, normed_hbm, out_sem)
    copy_out.start()
    for p in range(parts):
        copies[p].wait()
        part = pl.ds(p * rows, rows)
        logits_ref[part, :] = lax.dot_general(
            w_buf[part, :],
            normed_buf[...],
            (((1,), (1,)), ((), ())),
            preferred_element_type=jnp.float32,
        )
    logits = logits_ref[...]
    top = jnp.max(logits, axis=0, keepdims=True)
    exps = jnp.exp(logits - top)
    stats_ref[0:1, :] = top
    stats_ref[1:2, :] = jnp.sum(exps, axis=0, keepdims=True)
    stats_ref[2:3, :] = jnp.sum(target_ref[...] * logits, axis=0, keepdims=True)
    stats_ref[3:4, :] = jnp.sum(exps * logits, axis=0, keepdims=True)
    copy_out.wait()


def front(tokens_in, gain, weight_t, ids_t, teacher_t, labels, start):
    tokens, features = tokens_in.shape
    cols = weight_t.shape[0]
    parts = 3
    vmem = pl.BlockSpec(memory_space=pltpu.VMEM)
    hbm = pl.BlockSpec(memory_space=pltpu.HBM)
    return pl.pallas_call(
        front_kernel,
        name="front",
        out_shape=(
            jax.ShapeDtypeStruct((tokens, features), jnp.bfloat16),
            jax.ShapeDtypeStruct((tokens, 1), jnp.float32),
            jax.ShapeDtypeStruct((cols, tokens), jnp.float32),
            jax.ShapeDtypeStruct((cols, tokens), jnp.float32),
            jax.ShapeDtypeStruct((4, tokens), jnp.float32),
        ),
        in_specs=[pl.BlockSpec(memory_space=pltpu.SMEM), hbm, vmem, hbm, vmem, vmem, vmem],
        out_specs=(hbm, vmem, vmem, vmem, vmem),
        scratch_shapes=[
            pltpu.VMEM((tokens, features), jnp.bfloat16),
            pltpu.VMEM((cols, features), jnp.bfloat16),
            pltpu.VMEM((tokens, features), jnp.bfloat16),
            pltpu.SemaphoreType.DMA,
            pltpu.SemaphoreType.DMA((parts,)),
            pltpu.SemaphoreType.DMA,
        ],
        cost_estimate=pl.CostEstimate(
            flops=2 * tokens * features * cols,
            bytes_accessed=2 * features * (2 * tokens + cols),
            transcendentals=cols * tokens,
        ),
    )(start, tokens_in, gain, weight_t, ids_t, teacher_t, labels)


def back_kernel(dlogits_ref, w_ref, out_ref):
    width = out_ref.shape[2]
    for q in range(out_ref.shape[0]):
        out_ref[q] = jnp.dot(
            dlogits_ref[...],
            w_ref[:, q * width : (q + 1) * width],
            preferred_element_type=jnp.float32,
        ).astype(jnp.bfloat16)


def back(dlogits, weight_t, n_vocab):
    tokens, cols = dlogits.shape
    features = weight_t.shape[1]
    width = features // n_vocab
    group = 4
    return pl.pallas_call(
        back_kernel,
        name="back",
        grid=(n_vocab // group,),
        out_shape=jax.ShapeDtypeStruct((n_vocab, tokens, width), jnp.bfloat16),
        in_specs=[
            pl.BlockSpec((tokens, cols), lambda i: (0, 0)),
            pl.BlockSpec((cols, group * width), lambda i: (0, i)),
        ],
        out_specs=pl.BlockSpec((group, tokens, width), lambda i: (i, 0, 0)),
        cost_estimate=pl.CostEstimate(
            flops=2 * tokens * features * cols,
            bytes_accessed=2 * features * (tokens + cols),
            transcendentals=0,
        ),
    )(dlogits, weight_t)


def local(tokens_in, gain, head_weight, teacher_ids, teacher_weight, labels):
    tokens, features = tokens_in.shape
    col_width = head_weight.shape[1]
    n_vocab = NY * NX
    block = lax.axis_index("y") * NX + lax.axis_index("x")
    core = lax.axis_index("c")
    swap = [(0, 1), (1, 0)]
    weight_t = head_weight.T
    start = (block * col_width).astype(jnp.int32).reshape(1)
    normed, row_scale, logits, target, stats = front(
        tokens_in, gain[None], weight_t, teacher_ids.T, teacher_weight.T, labels[None], start
    )
    other_normed = lax.ppermute(normed, "c", swap)
    teacher_probs = teacher_weight / jnp.sum(teacher_weight, axis=1, keepdims=True)
    stats = lax.all_to_all(
        jnp.broadcast_to(stats[None], (n_vocab,) + stats.shape), ("y", "x"), 0, 0
    )
    row_top = jnp.max(stats[:, 0], axis=0)
    weight = jnp.exp(stats[:, 0] - row_top[None])
    total_exp = jnp.sum(weight * stats[:, 1], axis=0)
    total_dot = jnp.sum(stats[:, 2], axis=0)
    mean_logit = jnp.sum(weight * stats[:, 3], axis=0) / total_exp
    lse = row_top + jnp.log(total_exp)
    token_loss = (
        (1.0 - LABEL_SHARE) * jnp.sum(teacher_probs * jnp.log(teacher_probs), axis=1)
        - total_dot
        + lse
    )
    dlogits = (jnp.exp(logits - lse[None]) - target).astype(jnp.bfloat16)

    rows = col_width // (NZ * NC)
    by_owner = jnp.pad(dlogits.reshape(NZ, NC, rows, tokens), ((0, 0), (0, 0), (0, 2), (0, 0)))
    mine = lax.dynamic_index_in_dim(by_owner, core, 1, False).reshape(-1, tokens)
    theirs = lax.dynamic_index_in_dim(by_owner, 1 - core, 1, False).reshape(-1, tokens)
    other_mine = lax.ppermute(theirs, "c", swap)

    width = features // n_vocab
    pieces = back(dlogits.T, weight_t, n_vocab)
    pieces = lax.all_to_all(pieces, ("y", "x"), 0, 0)

    head_term = lax.dot_general(
        jnp.concatenate([mine, other_mine], axis=1),
        jnp.concatenate([normed, other_normed], axis=0),
        (((1,), (0,)), ((), ())),
        preferred_element_type=jnp.float32,
    )
    summed = lax.psum_scatter(head_term.astype(jnp.bfloat16), "z", scatter_dimension=0, tiled=True)
    head_grad = summed[:rows].astype(jnp.float32)[:, None, :]

    dhidden = jnp.sum(pieces.astype(jnp.float32), axis=0)
    local_tokens = lax.dynamic_slice_in_dim(tokens_in, block * width, width, 1).astype(jnp.float32)
    local_gain = lax.dynamic_slice_in_dim(gain, block * width, width, 0)
    inner_sum = row_scale * (mean_logit - total_dot)[:, None]
    cubed = row_scale * row_scale * row_scale
    grad_input = (
        dhidden * local_gain[None, :] / row_scale - local_tokens * inner_sum / (features * cubed)
    ).astype(jnp.bfloat16)
    return (token_loss, grad_input, head_grad)


def solution(mesh):
    fine = Mesh(mesh.devices.reshape(NZ, NC, NY, NX), ("z", "c", "y", "x"))
    dp, vocab = ("z", "c"), ("y", "x")
    in_specs = (P(dp, None), P(), P(None, vocab), P(dp, None), P(dp, None), P(dp))
    out_specs = (P(dp), P(dp, vocab), P(dp, vocab, None))
    return jax.shard_map(local, mesh=fine, in_specs=in_specs, out_specs=out_specs, check_vma=False)
```

time: 132 us -> 132 us (level)
  the two profiles are of different devices: /device:TPU:4 before, /device:TPU:2 now
where the time goes in v3:
time: 132 us
  waiting for transfers between devices  60.9 us (46%)
  starting transfers between devices  22.4 us (17%)
  Pallas kernels  18.8 us (14%)
  between operations  14.2 us (11%)
  local copies, waits for them, and re-layouts  6.28 us (5%)
  matrix products  5.16 us (4%)
  other arithmetic  3.86 us (3%)
    all_to_all x1, waiting for transfers between devices, local(): pieces = lax.all_to_all(pieces, ('y', 'x'), 0, 0)  48.9 us
    all_to_all x1, starting transfers between devices, local(): lax.all_to_all(jnp.broadcast_to(stats[None], (n_vocab,) + stats.shape), (...  13 us
    pallas_call x1, Pallas kernels, front(): pl.pallas_call(front_kernel, name='front', out_shape=(jax.ShapeDtypeStruc...  10.5 us
    pallas_call x1, Pallas kernels, back(): pl.pallas_call(back_kernel, name='back', grid=(n_vocab // group,), out_sh...  8.33 us
    all_to_all x1, waiting for transfers between devices, local(): lax.all_to_all(jnp.broadcast_to(stats[None], (n_vocab,) + stats.shape), (...  6.56 us
    all_to_all x1, starting transfers between devices, local(): pieces = lax.all_to_all(pieces, ('y', 'x'), 0, 0)  5.48 us
    dot_general x1, matrix products, local(): lax.dot_general(jnp.concatenate([mine, other_mine], axis=1), jnp.concaten...  5.16 us
    reduce_scatter x1, waiting for transfers between devices, local(): lax.psum_scatter(head_term.astype(jnp.bfloat16), 'z', scatter_dimension=0...  4.26 us
  transfers between devices with their start and end apart: 5, of which 4 were waited for; matrix products, arithmetic and copies ran while one was open for 6% of the time, Pallas kernels for 6%

profile of v3, /device:TPU:2, one launch (start us, length us, event | category | flops | bytes accessed | tf_op | source)
XLA Modules:
  0.0 131.6 jit_solution(369431388713789599)
XLA Ops:
  7.2 0.0 copy-start.1
  7.2 10.5 %front.1 = (bf16[128,8192]{1,0:T(8,128)(2,1)}, f32[128,1]{1,0:T(8,128)}, f32[528,128]{1,0:T(8,128)}, f32[528,128]{1,0:T(8,128)}, f32[4,128]{1,0:T(4,128)}) custom-call(s32[1]{0:T(128)} %bitcast.start_ref, bf16[128,8192]{1,0:T(8,128)(2,1)} %x_hbm.1, f32[1,8192]{1,0:T(1,128)} %bitcast.35, bf16[528,8192]{1,0:T(8,128)(2,1)} %bitcast.24, s32[16,128]{1,0:T(8,128)} %bitcast.36, ...), custom_call_target="tpu_custom_call" | custom-call | flops 1107296256 | bytes 12845056 | tf_op jit(solution)/shard_map/front/pallas_call | solution.py:82
  17.6 1.9 %collective-permute-start.1 = (bf16[128,8192]{1,0:T(8,128)(2,1)}, bf16[128,8192]{1,0:T(8,128)(2,1)S(1)}, u32[]{:S(2)}, u32[]{:S(2)}) collective-permute-start(bf16[128,8192]{1,0:T(8,128)(2,1)} %get-tuple-element.12), channel_id=1, source_target_pairs={{0,32},{32,0},{1,33},{33,1},{2,34},{34,2},{3,35},{35,3},{4,36},{36... | collective-permute-start | bytes 6291464 | tf_op jit(solution)/shard_map/ppermute | solution.py:155
  19.6 1.3 broadcast_in_dim.25
  20.9 13.0 %all-to-all-start = ((f32[32,4,128]{2,1,0:T(4,128)}), f32[32,4,128]{2,1,0:T(4,128)S(1)}, u32[]{:S(2)}, u32[]{:S(2)}) async-start(f32[32,4,128]{2,1,0:T(4,128)} %broadcast_in_dim.25), calls=%async_computation | async-start | bytes 131072 | tf_op jit(solution)/shard_map/all_to_all | solution.py:157
  33.9 0.0 reduce-scatter.2.cloned.1.call-start
  34.0 0.0 copy-done.1
  34.0 1.1 copy.38
  35.1 1.1 copy.40
  36.2 6.6 %all-to-all-done = f32[32,4,128]{2,1,0:T(4,128)S(1)} async-done(((f32[32,4,128]{2,1,0:T(4,128)}), f32[32,4,128]{2,1,0:T(4,128)S(1)}, u32[]{:S(2)}, u32[]{:S(2)}) %all-to-all-start) | async-done | bytes 65568 | tf_op jit(solution)/shard_map/all_to_all | solution.py:157
  42.9 0.5 subtract_add_fusion
  43.5 0.1 subtract_convert_fusion
  43.6 0.0 copy-start
  43.6 0.1 copy.42
  43.8 1.9 %collective-permute-start = (bf16[288,128]{1,0:T(8,128)(2,1)S(1)}, bf16[288,128]{1,0:T(8,128)(2,1)S(1)}, u32[]{:S(2)}, u32[]{:S(2)}) collective-permute-start(bf16[288,128]{1,0:T(8,128)(2,1)S(1)} %bitcast.30), channel_id=1, source_target_pairs={{0,32},{32,0},{1,33},{33,1},{2,34},{34,2},{3,35},{35,3},{4,36},{36... | collective-permute-start | bytes 221192 | tf_op jit(solution)/shard_map/ppermute | solution.py:177
  45.8 1.2 collective-permute-done
  47.0 0.0 collective-permute-done.1
  47.0 5.2 %convolution_convert_fusion = bf16[288,8192]{1,0:T(8,128)(2,1)} fusion(bf16[128,8192]{1,0:T(8,128)(2,1)S(1)} %collective-permute-done.1, bf16[128,8192]{1,0:T(8,128)(2,1)} %get-tuple-element.12, bf16[288,128]{1,0:T(8,128)(2,1)S(1)} %collective-permute-done, bf16[288,128]{1,0:T(8,128)(2,1)S(1)} %bitcast.29), kind=kOutput, calls=%fused_computation | convolution fusion | flops 1219002368 | bytes 9060352 | tf_op jit(solution)/shard_map/dot_general | solution.py:183
  52.2 0.0 copy-done
  52.2 0.0 reduce-scatter.2.cloned.1.call-update
  52.2 8.3 %back.1 = bf16[32,128,256]{2,1,0:T(8,128)(2,1)} custom-call(bf16[128,528]{1,0:T(8,128)(2,1)} %bitcast.26, bf16[528,8192]{1,0:T(8,128)(2,1)} %bitcast.25), custom_call_target="tpu_custom_call" | custom-call | flops 1107296256 | bytes 10747904 | tf_op jit(solution)/shard_map/back/pallas_call | solution.py:125
  60.5 5.5 %all-to-all-start.1 = ((bf16[32,128,256]{2,1,0:T(8,128)(2,1)}), bf16[32,128,256]{2,1,0:T(8,128)(2,1)S(1)}, u32[]{:S(2)}, u32[]{:S(2)}) async-start(bf16[32,128,256]{2,1,0:T(8,128)(2,1)} %back.1), calls=%async_computation.1 | async-start | bytes 4194304 | tf_op jit(solution)/shard_map/all_to_all | solution.py:181
  66.0 0.8 dynamic_slice.13
  66.8 0.1 copy.41
  66.9 0.0 copy-done.2
  66.9 0.1 fusion.11
  67.0 48.9 %all-to-all-done.1 = bf16[32,128,256]{2,1,0:T(8,128)(2,1)S(1)} async-done(((bf16[32,128,256]{2,1,0:T(8,128)(2,1)}), bf16[32,128,256]{2,1,0:T(8,128)(2,1)S(1)}, u32[]{:S(2)}, u32[]{:S(2)}) %all-to-all-start.1) | async-done | bytes 2097184 | tf_op jit(solution)/shard_map/all_to_all | solution.py:181
  115.9 0.3 convert_reduce_fusion
  116.2 1.6 %subtract_convert_fusion.1 = bf16[128,256]{1,0:T(8,128)(2,1)} fusion(f32[128,256]{1,0:T(8,128)S(1)} %convert_reduce_fusion, f32[128]{0:T(128)S(1)} %get-tuple-element.29, f32[128]{0:T(128)S(1)} %get-tuple-element.30, bf16[128,8192]{1,0:T(8,128)(2,1)} %x_hbm.1, s32[]{:T(128)S(6)} %select_n.11, f32[128]{0:T(128)S(1)} %get-tuple-element.28, ...), kind=kLoop, calls=%fused_computation.11 | loop fusion | flops 229376 | bytes 264708 | tf_op jit(solution)/shard_map/convert_element_type | solution.py:199
  117.8 4.3 %reduce-scatter.2.cloned.1.call-done = bf16[24,8192]{1,0:T(8,128)(2,1)} async-done(((bf16[288,8192]{1,0:T(8,128)(2,1)}), bf16[24,8192]{1,0:T(8,128)(2,1)}) %reduce-scatter.2.cloned.1.call-update) | async-done | bytes 393232 | tf_op jit(solution)/shard_map/reduce_scatter | solution.py:189
  122.1 1.0 fusion.3
  123.1 1.6 %copy.43 = f32[22,1,8192]{2,1,0:T(1,128)} copy(f32[22,1,8192]{2,0,1:T(8,128)S(1)} %fusion.3) | data formatting | bytes 1441792
  (9 shorter events, 0.2 us)
Async XLA Ops:
  7.2 26.8 %copy-start.1 = (f32[128,16]{0,1:T(8,128)S(1)}, f32[128,16]{0,1:T(8,128)}, u32[]{:S(2)}) copy-start(f32[128,16]{0,1:T(8,128)} %param.10) | copy-start | bytes 24580
  17.6 29.4 %collective-permute-start.1 = (bf16[128,8192]{1,0:T(8,128)(2,1)}, bf16[128,8192]{1,0:T(8,128)(2,1)S(1)}, u32[]{:S(2)}, u32[]{:S(2)}) collective-permute-start(bf16[128,8192]{1,0:T(8,128)(2,1)} %get-tuple-element.12), channel_id=1, source_target_pairs={{0,32},{32,0},{1,33},{33,1},{2,34},{34,2},{3,35},{35,3},{4,36},{36... | collective-permute-start | bytes 6291464 | tf_op jit(solution)/shard_map/ppermute | solution.py:155
  20.9 21.9 %all-to-all-start = ((f32[32,4,128]{2,1,0:T(4,128)}), f32[32,4,128]{2,1,0:T(4,128)S(1)}, u32[]{:S(2)}, u32[]{:S(2)}) async-start(f32[32,4,128]{2,1,0:T(4,128)} %broadcast_in_dim.25), calls=%async_computation | async-start | bytes 131072 | tf_op jit(solution)/shard_map/all_to_all | solution.py:157
  33.9 88.2 %reduce-scatter.2.cloned.1.call-start = ((), (), s32[]{:S(2)}) async-start(), calls=%async_computation.3 | async-start | bytes 5111808 | tf_op jit(solution)/shard_map/reduce_scatter | solution.py:189
  43.6 8.6 %copy-start = (bf16[528,128]{0,1:T(8,128)(2,1)}, bf16[528,128]{0,1:T(8,128)(2,1)S(1)}, u32[]{:S(2)}) copy-start(bf16[528,128]{0,1:T(8,128)(2,1)S(1)} %subtract_convert_fusion) | copy-start | bytes 405508
  43.8 3.2 %collective-permute-start = (bf16[288,128]{1,0:T(8,128)(2,1)S(1)}, bf16[288,128]{1,0:T(8,128)(2,1)S(1)}, u32[]{:S(2)}, u32[]{:S(2)}) collective-permute-start(bf16[288,128]{1,0:T(8,128)(2,1)S(1)} %bitcast.30), channel_id=1, source_target_pairs={{0,32},{32,0},{1,33},{33,1},{2,34},{34,2},{3,35},{35,3},{4,36},{36... | collective-permute-start | bytes 221192 | tf_op jit(solution)/shard_map/ppermute | solution.py:177
  60.5 6.4 %copy-start.2 = (f32[128,1]{1,0:T(8,128)S(1)}, f32[128,1]{1,0:T(8,128)}, u32[]{:S(2)}) copy-start(f32[128,1]{1,0:T(8,128)} %get-tuple-element.11) | copy-start | bytes 1540
  60.5 55.4 %all-to-all-start.1 = ((bf16[32,128,256]{2,1,0:T(8,128)(2,1)}), bf16[32,128,256]{2,1,0:T(8,128)(2,1)S(1)}, u32[]{:S(2)}, u32[]{:S(2)}) async-start(bf16[32,128,256]{2,1,0:T(8,128)(2,1)} %back.1), calls=%async_computation.1 | async-start | bytes 4194304 | tf_op jit(solution)/shard_map/all_to_all | solution.py:181
Sparse Core Ops, SparseCore 0:
  52.3 69.7 reduce-scatter.1

commit v4 on v3

v4 whole, which is shorter than its diff:
```python
import jax
import jax.numpy as jnp
from jax import lax
from jax.experimental import pallas as pl
from jax.experimental.pallas import tpu as pltpu
from jax.sharding import Mesh, PartitionSpec as P


LABEL_SHARE = 0.5
EPS = 1e-05
NZ, NC, NY, NX = 12, 2, 8, 4
SPLIT = 6144


def front_kernel(
    start_ref, x_hbm, gain_ref, w_hbm, ids_ref, weight_ref, label_ref,
    low_hbm, high_hbm, scale_ref, logits_ref, target_ref, stats_ref,
    x_buf, w_ref, normed_buf, x_sem, w_sem, out_sem,
):
    tokens, features = x_buf.shape
    cols = w_ref.shape[0]
    parts = w_sem.shape[0]
    rows = cols // parts
    lines = 16
    copy_x = pltpu.make_async_copy(x_hbm, x_buf, x_sem)
    copy_x.start()

    def copy_w(p):
        part = pl.ds(p * rows, rows)
        return pltpu.make_async_copy(w_hbm.at[part], w_ref.at[part], w_sem.at[p])

    @pl.loop(0, parts)
    def _(p):
        copy_w(p).start()

    probs = weight_ref[...] / jnp.sum(weight_ref[...], axis=0, keepdims=True)

    @pl.loop(0, cols // lines)
    def _(r):
        part = pl.ds(pl.multiple_of(r * lines, lines), lines)
        columns = start_ref[0] + r * lines + lax.broadcasted_iota(jnp.int32, (lines, tokens), 0)
        teacher_part = jnp.zeros((lines, tokens), jnp.float32)
        for k in range(ids_ref.shape[0]):
            teacher_part += jnp.where(ids_ref[k : k + 1, :] == columns, probs[k : k + 1, :], 0.0)
        label_part = jnp.where(label_ref[...] == columns, LABEL_SHARE, 0.0)
        target_ref[part, :] = (1.0 - LABEL_SHARE) * teacher_part + label_part

    copy_x.wait()

    @pl.loop(0, tokens // lines)
    def _(r):
        part = pl.ds(pl.multiple_of(r * lines, lines), lines)
        totals = [jnp.zeros((lines, 128), jnp.float32) for _ in range(4)]
        for f in range(0, features, 128):
            chunk = x_buf[part, f : f + 128].astype(jnp.float32)
            totals[f // 128 % 4] += chunk * chunk
        total = (totals[0] + totals[1]) + (totals[2] + totals[3])
        scale = jnp.sqrt(jnp.sum(total, axis=1, keepdims=True) / features + EPS)
        scale_ref[part, :] = scale
        inverse = jnp.broadcast_to(1.0 / scale, (lines, 128))
        for f in range(0, features, 128):
            chunk = x_buf[part, f : f + 128].astype(jnp.float32)
            chunk = chunk * inverse * gain_ref[:, f : f + 128]
            normed_buf[part, f : f + 128] = chunk.astype(jnp.bfloat16)

    copy_low = pltpu.make_async_copy(normed_buf.at[:, :SPLIT], low_hbm, out_sem.at[0])
    copy_high = pltpu.make_async_copy(normed_buf.at[:, SPLIT:], high_hbm, out_sem.at[1])
    copy_low.start()
    copy_high.start()
    for p in range(parts):
        copy_w(p).wait()
        part = pl.ds(p * rows, rows)
        logits_ref[part, :] = lax.dot_general(
            w_ref[part, :],
            normed_buf[...],
            (((1,), (1,)), ((), ())),
            preferred_element_type=jnp.float32,
        )
    logits = logits_ref[...]
    top = jnp.max(logits, axis=0, keepdims=True)
    exps = jnp.exp(logits - top)
    local_stats = (
        top,
        jnp.sum(exps, axis=0, keepdims=True),
        jnp.sum(target_ref[...] * logits, axis=0, keepdims=True),
        jnp.sum(exps * logits, axis=0, keepdims=True),
    )
    for q, row in enumerate(local_stats):
        stats_ref[:, q, :] = jnp.broadcast_to(row, (stats_ref.shape[0], tokens))
    copy_low.wait()
    copy_high.wait()


def front(tokens_in, gain, weight_t, ids_t, teacher_t, labels, start, n_vocab):
    tokens, features = tokens_in.shape
    cols = weight_t.shape[0]
    parts = 3
    vmem = pl.BlockSpec(memory_space=pltpu.VMEM)
    hbm = pl.BlockSpec(memory_space=pltpu.HBM)
    return pl.pallas_call(
        front_kernel,
        name="front",
        out_shape=(
            jax.ShapeDtypeStruct((tokens, SPLIT), jnp.bfloat16),
            jax.ShapeDtypeStruct((tokens, features - SPLIT), jnp.bfloat16),
            jax.ShapeDtypeStruct((tokens, 1), jnp.float32),
            jax.ShapeDtypeStruct((cols, tokens), jnp.float32),
            jax.ShapeDtypeStruct((cols, tokens), jnp.float32),
            jax.ShapeDtypeStruct((n_vocab, 4, tokens), jnp.float32),
        ),
        in_specs=[pl.BlockSpec(memory_space=pltpu.SMEM), hbm, vmem, hbm, vmem, vmem, vmem],
        out_specs=(hbm, hbm, vmem, vmem, vmem, vmem),
        scratch_shapes=[
            pltpu.VMEM((tokens, features), jnp.bfloat16),
            pltpu.VMEM((cols, features), jnp.bfloat16),
            pltpu.VMEM((tokens, features), jnp.bfloat16),
            pltpu.SemaphoreType.DMA,
            pltpu.SemaphoreType.DMA((parts,)),
            pltpu.SemaphoreType.DMA((2,)),
        ],
        cost_estimate=pl.CostEstimate(
            flops=2 * tokens * features * cols,
            bytes_accessed=2 * features * (2 * tokens + cols),
            transcendentals=cols * tokens,
        ),
    )(start, tokens_in, gain, weight_t, ids_t, teacher_t, labels)


def local(tokens_in, gain, head_weight, teacher_ids, teacher_weight, labels):
    tokens, features = tokens_in.shape
    col_width = head_weight.shape[1]
    n_vocab = NY * NX
    block = lax.axis_index("y") * NX + lax.axis_index("x")
    core = lax.axis_index("c")
    swap = [(0, 1), (1, 0)]
    weight_t = head_weight.T
    start = (block * col_width).astype(jnp.int32).reshape(1)
    low, high, row_scale, logits, target, stats = front(
        tokens_in, gain[None], weight_t, teacher_ids.T, teacher_weight.T, labels[None], start, n_vocab
    )
    both_low = jnp.concatenate([low, lax.ppermute(low, "c", swap)], axis=0)
    both_high = jnp.concatenate([high, lax.ppermute(high, "c", swap)], axis=0)
    teacher_probs = teacher_weight / jnp.sum(teacher_weight, axis=1, keepdims=True)
    stats = lax.all_to_all(stats, ("y", "x"), 0, 0)
    row_top = jnp.max(stats[:, 0], axis=0)
    weight = jnp.exp(stats[:, 0] - row_top[None])
    total_exp = jnp.sum(weight * stats[:, 1], axis=0)
    total_dot = jnp.sum(stats[:, 2], axis=0)
    mean_logit = jnp.sum(weight * stats[:, 3], axis=0) / total_exp
    lse = row_top + jnp.log(total_exp)
    token_loss = (
        (1.0 - LABEL_SHARE) * jnp.sum(teacher_probs * jnp.log(teacher_probs), axis=1)
        - total_dot
        + lse
    )
    dlogits = (jnp.exp(logits - lse[None]) - target).astype(jnp.bfloat16)

    rows = col_width // (NZ * NC)
    by_owner = jnp.pad(dlogits.reshape(NZ, NC, rows, tokens), ((0, 0), (0, 0), (0, 2), (0, 0)))
    mine = lax.dynamic_index_in_dim(by_owner, core, 1, False).reshape(-1, tokens)
    theirs = lax.dynamic_index_in_dim(by_owner, 1 - core, 1, False).reshape(-1, tokens)
    other_mine = lax.ppermute(theirs, "c", swap)

    width = features // n_vocab
    partial_value = lax.dot_general(
        dlogits, weight_t, (((0,), (0,)), ((), ())), preferred_element_type=jnp.float32
    ).astype(jnp.bfloat16)
    pieces = partial_value.reshape(tokens, n_vocab, width).transpose(1, 0, 2)
    pieces = lax.all_to_all(pieces, ("y", "x"), 0, 0)

    factor = jnp.concatenate([mine, other_mine], axis=1)
    term1 = jnp.dot(factor, both_low, preferred_element_type=jnp.float32)
    summed1 = lax.psum_scatter(
        term1.astype(jnp.bfloat16), "z", scatter_dimension=0, tiled=True
    )[:rows]
    packed = factor.reshape(NZ, -1, 2 * tokens)[:, :rows].reshape(NZ * rows, 2 * tokens)
    term2 = jnp.dot(packed, both_high, preferred_element_type=jnp.float32)
    summed2 = lax.psum_scatter(
        term2.astype(jnp.bfloat16), "z", scatter_dimension=0, tiled=True
    )
    head_grad = jnp.concatenate([summed1, summed2], axis=1).astype(jnp.float32)[:, None, :]

    dhidden = jnp.sum(pieces.astype(jnp.float32), axis=0)
    local_tokens = lax.dynamic_slice_in_dim(tokens_in, block * width, width, 1).astype(jnp.float32)
    local_gain = lax.dynamic_slice_in_dim(gain, block * width, width, 0)
    inner_sum = row_scale * (mean_logit - total_dot)[:, None]
    cubed = row_scale * row_scale * row_scale
    grad_input = (
        dhidden * local_gain[None, :] / row_scale - local_tokens * inner_sum / (features * cubed)
    ).astype(jnp.bfloat16)
    return (token_loss, grad_input, head_grad)


def solution(mesh):
    fine = Mesh(mesh.devices.reshape(NZ, NC, NY, NX), ("z", "c", "y", "x"))
    dp, vocab = ("z", "c"), ("y", "x")
    in_specs = (P(dp, None), P(), P(None, vocab), P(dp, None), P(dp, None), P(dp))
    out_specs = (P(dp), P(dp, vocab), P(dp, vocab, None))
    return jax.shard_map(local, mesh=fine, in_specs=in_specs, out_specs=out_specs, check_vma=False)
```

time: 132 us -> 133 us (level)
  waiting for transfers between devices: 60.9 us -> 12.9 us
  blocking collectives: 0 us -> 46.1 us
  Pallas kernels: 18.8 us -> 9.01 us
  matrix products: 5.16 us -> 11.3 us
  starting transfers between devices: 22.4 us -> 27.2 us
    all_to_all x1, waiting for transfers between devices: 48.9 us -> 0.01 us  [local(): pieces = lax.all_to_all(pieces, ('y', 'x'), 0, 0)]
    unnamed x0 -> x1, blocking collectives: none -> 46.1 us
    pallas_call x1 -> x0, Pallas kernels: 8.33 us -> none  [back(): pl.pallas_call(back_kernel, name='back', grid=(n_vocab // group,), out_sh...]
    dot_general x1 -> x3, matrix products: 5.16 us -> 11.3 us  [the longest x1 5.32 us: local(): lax.dot_general(dlogits, weight_t, (((0,), (0,)), ((), ())), preferred_el...]
    reduce_scatter x1, waiting for transfers between devices: 4.26 us -> 0.65 us  [local(): lax.psum_scatter(term1.astype(jnp.bfloat16), 'z', scatter_dimension=0, ti...]
    unnamed x0 -> x1, starting transfers between devices: none -> 2.93 us
    all_to_all x1, waiting for transfers between devices: 6.56 us -> 8.8 us  [local(): stats = lax.all_to_all(stats, ('y', 'x'), 0, 0)]
    pallas_call x2 -> x0, local copies, waits for them, and re-layouts: 2.23 us -> none  [front(): pl.pallas_call(front_kernel, name='front', out_shape=(jax.ShapeDtypeStruc...]
  transfers between devices with their start and end apart: 5 -> 7, of which waited for: 4 -> 4; matrix products, arithmetic and copies ran while one was open for 6% -> 46% of each run, Pallas kernels for 6% -> 0%
where the time goes in v4:
time: 133 us; the launch traced here: 132 us
  blocking collectives  46.1 us (35%)
  starting transfers between devices  27.2 us (20%)
  between operations  14.9 us (11%)
  waiting for transfers between devices  12.9 us (10%)
  matrix products  11.3 us (8%)
  Pallas kernels  9.01 us (7%)
  local copies, waits for them, and re-layouts  6.76 us (5%)
  other arithmetic  3.88 us (3%)
    unnamed x1, blocking collectives  46.1 us
    all_to_all x1, starting transfers between devices, local(): stats = lax.all_to_all(stats, ('y', 'x'), 0, 0)  13 us
    pallas_call x1, Pallas kernels, front(): pl.pallas_call(front_kernel, name='front', out_shape=(jax.ShapeDtypeStruc...  9.01 us
    all_to_all x1, waiting for transfers between devices, local(): stats = lax.all_to_all(stats, ('y', 'x'), 0, 0)  8.8 us
    all_to_all x1, starting transfers between devices, local(): pieces = lax.all_to_all(pieces, ('y', 'x'), 0, 0)  5.48 us
    dot_general x1, matrix products, local(): lax.dot_general(dlogits, weight_t, (((0,), (0,)), ((), ())), preferred_el...  5.32 us
    dot_general x1, matrix products, local(): term1 = jnp.dot(factor, both_low, preferred_element_type=jnp.float32)  4.27 us
    unnamed x10, local copies, waits for them, and re-layouts  3.13 us
  transfers between devices with their start and end apart: 7, of which 4 were waited for; matrix products, arithmetic and copies ran while one was open for 46% of the time, Pallas kernels for 0%

profile of v4, /device:TPU:2, one launch (start us, length us, event | category | flops | bytes accessed | tf_op | source)
XLA Modules:
  0.0 132.0 jit_solution(8450820887828939146)
XLA Ops:
  7.2 9.0 %front.1 = (bf16[128,6144]{1,0:T(8,128)(2,1)}, bf16[128,2048]{1,0:T(8,128)(2,1)}, f32[128,1]{1,0:T(8,128)}, f32[528,128]{1,0:T(8,128)}, f32[528,128]{1,0:T(8,128)}, /*index=5*/f32[32,4,128]{2,1,0:T(4,128)}) custom-call(s32[1]{0:T(128)} %bitcast.start_ref, bf16[128,8192]{1,0:T(8,128)(2,1)} %x_hbm.1, f32[1,8192]{1,0:T(1,128)} %bitcast.48, ...), custom_call_target="tpu_custom_call" | custom-call | flops 1107296256 | bytes 12845056 | tf_op jit(solution)/shard_map/front/pallas_call | solution.py:100
  16.2 1.9 %collective-permute-start.1 = (bf16[128,6144]{1,0:T(8,128)(2,1)}, bf16[128,6144]{1,0:T(8,128)(2,1)S(1)}, u32[]{:S(2)}, u32[]{:S(2)}) collective-permute-start(bf16[128,6144]{1,0:T(8,128)(2,1)} %get-tuple-element.13), channel_id=1, source_target_pairs={{0,32},{32,0},{1,33},{33,1},{2,34},{34,2},{3,35},{35,3},{4,36},{36... | collective-permute-start | bytes 4718600 | tf_op jit(solution)/shard_map/ppermute | solution.py:141
  18.1 13.0 %all-to-all-start = ((f32[32,4,128]{2,1,0:T(4,128)}), f32[32,4,128]{2,1,0:T(4,128)S(1)}, u32[]{:S(2)}, u32[]{:S(2)}) async-start(f32[32,4,128]{2,1,0:T(4,128)} %get-tuple-element.9), calls=%async_computation | async-start | bytes 131072 | tf_op jit(solution)/shard_map/all_to_all | solution.py:144
  31.2 0.0 reduce-scatter.4.cloned.1.call-start
  31.3 8.8 %all-to-all-done = f32[32,4,128]{2,1,0:T(4,128)S(1)} async-done(((f32[32,4,128]{2,1,0:T(4,128)}), f32[32,4,128]{2,1,0:T(4,128)S(1)}, u32[]{:S(2)}, u32[]{:S(2)}) %all-to-all-start) | async-done | bytes 65568 | tf_op jit(solution)/shard_map/all_to_all | solution.py:144
  40.1 0.1 fusion.16
  40.2 0.5 subtract_add_fusion
  40.7 1.1 subtract_convert_fusion
  41.9 1.9 %collective-permute-start = (bf16[288,128]{1,0:T(8,128)(2,1)S(1)}, bf16[288,128]{1,0:T(8,128)(2,1)S(1)}, u32[]{:S(2)}, u32[]{:S(2)}) collective-permute-start(bf16[288,128]{1,0:T(8,128)(2,1)S(1)} %bitcast.44), channel_id=1, source_target_pairs={{0,32},{32,0},{1,33},{33,1},{2,34},{34,2},{3,35},{35,3},{4,36},{36... | collective-permute-start | bytes 221192 | tf_op jit(solution)/shard_map/ppermute | solution.py:162
  43.8 1.2 collective-permute-done
  45.1 4.3 %convolution_convert_fusion.1 = bf16[288,6144]{1,0:T(8,128)(2,1)} fusion(bf16[128,6144]{1,0:T(8,128)(2,1)S(1)} %collective-permute-done.1, bf16[128,6144]{1,0:T(8,128)(2,1)} %get-tuple-element.13, bf16[288,128]{1,0:T(8,128)(2,1)S(1)} %collective-permute-done, bf16[288,128]{1,0:T(8,128)(2,1)S(1)} %bitcast.39), kind=kOutput, calls=%fused_computation.1 | convolution fusion | flops 914325504 | bytes 6832128 | tf_op jit(solution)/shard_map/dot_general | solution.py:172
  49.3 0.0 reduce-scatter.4.cloned.1.call-update
  49.3 5.3 %convolution_convert_fusion = bf16[128,8192]{1,0:T(8,128)(2,1)S(1)} fusion(bf16[528,128]{1,0:T(8,128)(2,1)S(1)} %subtract_convert_fusion, bf16[8192,528]{0,1:T(8,128)(2,1)} %param.8), kind=kOutput, calls=%fused_computation | convolution fusion | flops 1108344832 | bytes 10883072 | tf_op jit(solution)/shard_map/dot_general | solution.py:165
  54.7 1.6 %copy.26 = bf16[16,32,8,256]{3,2,0,1:T(8,128)(2,1)} copy(bf16[16,32,8,256]{3,2,1,0:T(8,128)(2,1)S(1)} %bitcast.37) | data formatting | bytes 4194304 | tf_op jit(solution)/shard_map/reshape | solution.py:168
  56.3 5.5 %all-to-all-start.1 = ((bf16[32,128,256]{2,1,0:T(8,128)(2,1)}), bf16[32,128,256]{2,1,0:T(8,128)(2,1)S(1)}, u32[]{:S(2)}, u32[]{:S(2)}) async-start(bf16[32,128,256]{2,1,0:T(8,128)(2,1)} %bitcast.38), calls=%async_computation.1 | async-start | bytes 4194304 | tf_op jit(solution)/shard_map/all_to_all | solution.py:169
  61.8 1.9 %collective-permute-start.2 = (bf16[128,2048]{1,0:T(8,128)(2,1)S(1)}, bf16[128,2048]{1,0:T(8,128)(2,1)}, u32[]{:S(2)}, u32[]{:S(2)}) collective-permute-start(bf16[128,2048]{1,0:T(8,128)(2,1)S(1)} %copy-done), channel_id=1, source_target_pairs={{0,32},{32,0},{1,33},{33,1},{2,34},{34,2},{3,35},{35,3},{4,36},{36... | collective-permute-start | bytes 1572872 | tf_op jit(solution)/shard_map/ppermute | solution.py:142
  63.7 0.8 dynamic_slice.13
  64.5 1.3 dynamic-slice.4
  66.4 0.1 copy.20
  66.6 0.0 copy-start.2
  66.6 1.7 %convolution_convert_fusion.2 = bf16[264,2048]{1,0:T(8,128)(2,1)S(1)} fusion(bf16[264,256]{1,0:T(8,128)(2,1)S(1)} %reshape.93, bf16[128,2048]{1,0:T(8,128)(2,1)} %collective-permute-done.2, bf16[128,2048]{1,0:T(8,128)(2,1)} %get-tuple-element.14), kind=kOutput, calls=%fused_computation.6 | convolution fusion | flops 279461888 | bytes 2265088 | tf_op jit(solution)/shard_map/dot_general | solution.py:177
  68.3 46.1 %fusion = bf16[24,2048]{1,0:T(8,128)(2,1)S(1)} fusion(bf16[264,2048]{1,0:T(8,128)(2,1)S(1)} %convolution_convert_fusion.2), kind=kCustom, calls=%all-reduce-scatter | all-reduce-scatter fusion | flops 589825 | bytes 1183744
  114.5 2.9 %collective-permute-start.3 = (bf16[22,2048]{1,0:T(8,128)(2,1)S(1)}, bf16[22,2048]{1,0:T(8,128)(2,1)S(1)}, u32[]{:S(2)}, u32[]{:S(2)}) collective-permute-start(bf16[22,2048]{1,0:T(8,128)(2,1)S(1)} %slice.30), channel_id=1, source_target_pairs={{0,64},{64,128},{128,192},{192,256},{256,320},{320,384},{384,448},... | collective-permute-start | bytes 270344
  117.4 0.1 fusion.15
  117.5 2.2 %collective-permute-done.3 = bf16[22,2048]{1,0:T(8,128)(2,1)S(1)} collective-permute-done((bf16[22,2048]{1,0:T(8,128)(2,1)S(1)}, bf16[22,2048]{1,0:T(8,128)(2,1)S(1)}, u32[]{:S(2)}, u32[]{:S(2)}) %collective-permute-start.3) | collective-permute-done | bytes 90144
  119.7 0.2 concatenate.39
  120.0 0.3 convert_reduce_fusion
  120.3 1.6 %subtract_convert_fusion.1 = bf16[128,256]{1,0:T(8,128)(2,1)} fusion(f32[128,256]{1,0:T(8,128)S(1)} %convert_reduce_fusion, f32[128]{0:T(128)S(1)} %get-tuple-element.25, f32[128]{0:T(128)S(1)} %get-tuple-element.26, bf16[128,8192]{1,0:T(8,128)(2,1)} %x_hbm.1, s32[]{:T(128)S(6)} %select_n.11, f32[128]{0:T(128)S(1)} %get-tuple-element.24, ...), kind=kLoop, calls=%fused_computation.18 | loop fusion | flops 229376 | bytes 264708 | tf_op jit(solution)/shard_map/convert_element_type | solution.py:190
  121.9 0.7 reduce-scatter.4.cloned.1.call-done
  122.5 1.0 slice_bitcast_fusion
  123.5 0.1 maximum_convert_fusion
  123.6 1.6 %copy.21 = f32[22,1,8192]{2,1,0:T(1,128)} copy(f32[22,1,8192]{2,0,1:T(8,128)S(1)} %maximum_convert_fusion) | data formatting | bytes 1441792
  (18 shorter events, 0.3 us)
Async XLA Ops:
  7.2 24.0 %copy-start.1 = (f32[128,16]{0,1:T(8,128)S(1)}, f32[128,16]{0,1:T(8,128)}, u32[]{:S(2)}) copy-start(f32[128,16]{0,1:T(8,128)} %param.10) | copy-start | bytes 24580
  16.2 28.9 %collective-permute-start.1 = (bf16[128,6144]{1,0:T(8,128)(2,1)}, bf16[128,6144]{1,0:T(8,128)(2,1)S(1)}, u32[]{:S(2)}, u32[]{:S(2)}) collective-permute-start(bf16[128,6144]{1,0:T(8,128)(2,1)} %get-tuple-element.13), channel_id=1, source_target_pairs={{0,32},{32,0},{1,33},{33,1},{2,34},{34,2},{3,35},{35,3},{4,36},{36... | collective-permute-start | bytes 4718600 | tf_op jit(solution)/shard_map/ppermute | solution.py:141
  18.1 21.9 %all-to-all-start = ((f32[32,4,128]{2,1,0:T(4,128)}), f32[32,4,128]{2,1,0:T(4,128)S(1)}, u32[]{:S(2)}, u32[]{:S(2)}) async-start(f32[32,4,128]{2,1,0:T(4,128)} %get-tuple-element.9), calls=%async_computation | async-start | bytes 131072 | tf_op jit(solution)/shard_map/all_to_all | solution.py:144
  31.2 91.4 %reduce-scatter.4.cloned.1.call-start = ((), (), s32[]{:S(2)}) async-start(), calls=%async_computation.3 | async-start | bytes 3833856 | tf_op jit(solution)/shard_map/reduce_scatter | solution.py:173
  41.9 3.2 %collective-permute-start = (bf16[288,128]{1,0:T(8,128)(2,1)S(1)}, bf16[288,128]{1,0:T(8,128)(2,1)S(1)}, u32[]{:S(2)}, u32[]{:S(2)}) collective-permute-start(bf16[288,128]{1,0:T(8,128)(2,1)S(1)} %bitcast.44), channel_id=1, source_target_pairs={{0,32},{32,0},{1,33},{33,1},{2,34},{34,2},{3,35},{35,3},{4,36},{36... | collective-permute-start | bytes 221192 | tf_op jit(solution)/shard_map/ppermute | solution.py:162
  56.3 5.5 %copy-start = (bf16[128,2048]{1,0:T(8,128)(2,1)S(1)}, bf16[128,2048]{1,0:T(8,128)(2,1)}, u32[]{:S(2)}) copy-start(bf16[128,2048]{1,0:T(8,128)(2,1)} %get-tuple-element.14) | copy-start | bytes 1572868
  56.3 63.7 %all-to-all-start.1 = ((bf16[32,128,256]{2,1,0:T(8,128)(2,1)}), bf16[32,128,256]{2,1,0:T(8,128)(2,1)S(1)}, u32[]{:S(2)}, u32[]{:S(2)}) async-start(bf16[32,128,256]{2,1,0:T(8,128)(2,1)} %bitcast.38), calls=%async_computation.1 | async-start | bytes 4194304 | tf_op jit(solution)/shard_map/all_to_all | solution.py:169
  61.8 4.8 %collective-permute-start.2 = (bf16[128,2048]{1,0:T(8,128)(2,1)S(1)}, bf16[128,2048]{1,0:T(8,128)(2,1)}, u32[]{:S(2)}, u32[]{:S(2)}) collective-permute-start(bf16[128,2048]{1,0:T(8,128)(2,1)S(1)} %copy-done), channel_id=1, source_target_pairs={{0,32},{32,0},{1,33},{33,1},{2,34},{34,2},{3,35},{35,3},{4,36},{36... | collective-permute-start | bytes 1572872 | tf_op jit(solution)/shard_map/ppermute | solution.py:142
  66.6 50.8 %copy-start.2 = (f32[128,1]{1,0:T(8,128)S(1)}, f32[128,1]{1,0:T(8,128)}, u32[]{:S(2)}) copy-start(f32[128,1]{1,0:T(8,128)} %get-tuple-element.12) | copy-start | bytes 1540
  114.5 5.3 %collective-permute-start.3 = (bf16[22,2048]{1,0:T(8,128)(2,1)S(1)}, bf16[22,2048]{1,0:T(8,128)(2,1)S(1)}, u32[]{:S(2)}, u32[]{:S(2)}) collective-permute-start(bf16[22,2048]{1,0:T(8,128)(2,1)S(1)} %slice.30), channel_id=1, source_target_pairs={{0,64},{64,128},{128,192},{192,256},{256,320},{320,384},{384,448},... | collective-permute-start | bytes 270344
Sparse Core Ops, SparseCore 0:
  49.5 73.0 reduce-scatter.3

commit v5 on v4

--- a/solution.py
+++ b/solution.py
@@ -9,29 +9,28 @@
 LABEL_SHARE = 0.5
 EPS = 1e-05
 NZ, NC, NY, NX = 12, 2, 8, 4
-SPLIT = 6144
 
 
 def front_kernel(
     start_ref, x_hbm, gain_ref, w_hbm, ids_ref, weight_ref, label_ref,
-    low_hbm, high_hbm, scale_ref, logits_ref, target_ref, stats_ref,
+    normed_hbm, scale_ref, logits_ref, target_ref, stats_ref,
     x_buf, w_ref, normed_buf, x_sem, w_sem, out_sem,
 ):
     tokens, features = x_buf.shape
     cols = w_ref.shape[0]
-    parts = w_sem.shape[0]
-    rows = cols // parts
+    bounds = (0, 240, 432, cols)
     lines = 16
     copy_x = pltpu.make_async_copy(x_hbm, x_buf, x_sem)
     copy_x.start()
 
     def copy_w(p):
-        part = pl.ds(p * rows, rows)
+        part = pl.ds(bounds[p], bounds[p + 1] - bounds[p])
         return pltpu.make_async_copy(w_hbm.at[part], w_ref.at[part], w_sem.at[p])
 
-    @pl.loop(0, parts)
-    def _(p):
-        copy_w(p).start()
+    @pl.when(start_ref[0] >= 0)
+    def _():
+        for p in range(len(bounds) - 1):
+            copy_w(p).start()
 
     probs = weight_ref[...] / jnp.sum(weight_ref[...], axis=0, keepdims=True)
 
@@ -63,13 +62,11 @@
             chunk = chunk * inverse * gain_ref[:, f : f + 128]
             normed_buf[part, f : f + 128] = chunk.astype(jnp.bfloat16)
 
-    copy_low = pltpu.make_async_copy(normed_buf.at[:, :SPLIT], low_hbm, out_sem.at[0])
-    copy_high = pltpu.make_async_copy(normed_buf.at[:, SPLIT:], high_hbm, out_sem.at[1])
-    copy_low.start()
-    copy_high.start()
-    for p in range(parts):
+    copy_out = pltpu.make_async_copy(normed_buf, normed_hbm, out_sem)
+    copy_out.start()
+    for p in range(len(bounds) - 1):
         copy_w(p).wait()
-        part = pl.ds(p * rows, rows)
+        part = pl.ds(bounds[p], bounds[p + 1] - bounds[p])
         logits_ref[part, :] = lax.dot_general(
             w_ref[part, :],
             normed_buf[...],
@@ -87,36 +84,33 @@
     )
     for q, row in enumerate(local_stats):
         stats_ref[:, q, :] = jnp.broadcast_to(row, (stats_ref.shape[0], tokens))
-    copy_low.wait()
-    copy_high.wait()
+    copy_out.wait()
 
 
 def front(tokens_in, gain, weight_t, ids_t, teacher_t, labels, start, n_vocab):
     tokens, features = tokens_in.shape
     cols = weight_t.shape[0]
-    parts = 3
     vmem = pl.BlockSpec(memory_space=pltpu.VMEM)
     hbm = pl.BlockSpec(memory_space=pltpu.HBM)
     return pl.pallas_call(
         front_kernel,
         name="front",
         out_shape=(
-            jax.ShapeDtypeStruct((tokens, SPLIT), jnp.bfloat16),
-            jax.ShapeDtypeStruct((tokens, features - SPLIT), jnp.bfloat16),
+            jax.ShapeDtypeStruct((tokens, features), jnp.bfloat16),
             jax.ShapeDtypeStruct((tokens, 1), jnp.float32),
             jax.ShapeDtypeStruct((cols, tokens), jnp.float32),
             jax.ShapeDtypeStruct((cols, tokens), jnp.float32),
             jax.ShapeDtypeStruct((n_vocab, 4, tokens), jnp.float32),
         ),
         in_specs=[pl.BlockSpec(memory_space=pltpu.SMEM), hbm, vmem, hbm, vmem, vmem, vmem],
-        out_specs=(hbm, hbm, vmem, vmem, vmem, vmem),
+        out_specs=(hbm, vmem, vmem, vmem, vmem),
         scratch_shapes=[
             pltpu.VMEM((tokens, features), jnp.bfloat16),
             pltpu.VMEM((cols, features), jnp.bfloat16),
             pltpu.VMEM((tokens, features), jnp.bfloat16),
             pltpu.SemaphoreType.DMA,
-            pltpu.SemaphoreType.DMA((parts,)),
-            pltpu.SemaphoreType.DMA((2,)),
+            pltpu.SemaphoreType.DMA((3,)),
+            pltpu.SemaphoreType.DMA,
         ],
         cost_estimate=pl.CostEstimate(
             flops=2 * tokens * features * cols,
@@ -124,6 +118,29 @@
             transcendentals=cols * tokens,
         ),
     )(start, tokens_in, gain, weight_t, ids_t, teacher_t, labels)
+
+
+def spread_kernel(in_ref, out_ref):
+    for r in range(out_ref.shape[0]):
+        if r % 8 == 0:
+            lines = in_ref[r : r + 8, :].astype(jnp.float32)
+        out_ref[r] = lines[r % 8 : r % 8 + 1, :]
+
+
+def spread(summed, rows):
+    features = summed.shape[1]
+    step = 2048
+    return pl.pallas_call(
+        spread_kernel,
+        name="spread",
+        grid=(features // step,),
+        out_shape=jax.ShapeDtypeStruct((rows, 1, features), jnp.float32),
+        in_specs=[pl.BlockSpec((summed.shape[0], step), lambda i: (0, i))],
+        out_specs=pl.BlockSpec((rows, 1, step), lambda i: (0, 0, i)),
+        cost_estimate=pl.CostEstimate(
+            flops=0, bytes_accessed=8 * rows * features, transcendentals=0
+        ),
+    )(summed)
 
 
 def local(tokens_in, gain, head_weight, teacher_ids, teacher_weight, labels):
@@ -135,11 +152,10 @@
     swap = [(0, 1), (1, 0)]
     weight_t = head_weight.T
     start = (block * col_width).astype(jnp.int32).reshape(1)
-    low, high, row_scale, logits, target, stats = front(
+    normed, row_scale, logits, target, stats = front(
         tokens_in, gain[None], weight_t, teacher_ids.T, teacher_weight.T, labels[None], start, n_vocab
     )
-    both_low = jnp.concatenate([low, lax.ppermute(low, "c", swap)], axis=0)
-    both_high = jnp.concatenate([high, lax.ppermute(high, "c", swap)], axis=0)
+    both = jnp.concatenate([normed, lax.ppermute(normed, "c", swap)], axis=0)
     teacher_probs = teacher_weight / jnp.sum(teacher_weight, axis=1, keepdims=True)
     stats = lax.all_to_all(stats, ("y", "x"), 0, 0)
     row_top = jnp.max(stats[:, 0], axis=0)
@@ -169,16 +185,9 @@
     pieces = lax.all_to_all(pieces, ("y", "x"), 0, 0)
 
     factor = jnp.concatenate([mine, other_mine], axis=1)
-    term1 = jnp.dot(factor, both_low, preferred_element_type=jnp.float32)
-    summed1 = lax.psum_scatter(
-        term1.astype(jnp.bfloat16), "z", scatter_dimension=0, tiled=True
-    )[:rows]
-    packed = factor.reshape(NZ, -1, 2 * tokens)[:, :rows].reshape(NZ * rows, 2 * tokens)
-    term2 = jnp.dot(packed, both_high, preferred_element_type=jnp.float32)
-    summed2 = lax.psum_scatter(
-        term2.astype(jnp.bfloat16), "z", scatter_dimension=0, tiled=True
-    )
-    head_grad = jnp.concatenate([summed1, summed2], axis=1).astype(jnp.float32)[:, None, :]
+    head_term = jnp.dot(factor, both, preferred_element_type=jnp.float32)
+    summed = lax.psum_scatter(head_term.astype(jnp.bfloat16), "z", scatter_dimension=0, tiled=True)
+    head_grad = spread(summed, rows)
 
     dhidden = jnp.sum(pieces.astype(jnp.float32), axis=0)
     local_tokens = lax.dynamic_slice_in_dim(tokens_in, block * width, width, 1).astype(jnp.float32)

time: 133 us -> 132 us (level)
  waiting for transfers between devices: 12.9 us -> 64.6 us
  blocking collectives: 46.1 us -> 0 us
  starting transfers between devices: 27.2 us -> 22.2 us
  local copies, waits for them, and re-layouts: 6.76 us -> 2.59 us
  Pallas kernels: 9.01 us -> 12.9 us
    all_to_all x1, waiting for transfers between devices: 0.01 us -> 48.9 us  [local(): pieces = lax.all_to_all(pieces, ('y', 'x'), 0, 0)]
    unnamed x1 -> x0, blocking collectives: 46.1 us -> none
    reduce_scatter x1, waiting for transfers between devices: 0.65 us -> 5.71 us  [local(): lax.psum_scatter(head_term.astype(jnp.bfloat16), 'z', scatter_dimension=0...]
    pallas_call x0 -> x1, Pallas kernels: none -> 3.22 us  [spread(): pl.pallas_call(spread_kernel, name='spread', grid=(features // step,), ou...]
    unnamed x10 -> x4, local copies, waits for them, and re-layouts: 3.13 us -> 0.01 us
    unnamed x1 -> x0, starting transfers between devices: 2.93 us -> none
    unnamed x2 -> x1, waiting for transfers between devices: 2.19 us -> 0.02 us
    ppermute x2 -> x1, starting transfers between devices: 3.84 us -> 1.92 us  [local(): both = jnp.concatenate([normed, lax.ppermute(normed, 'c', swap)], axis=0)]
  transfers between devices with their start and end apart: 7 -> 5, of which waited for: 4 -> 4; matrix products, arithmetic and copies ran while one was open for 46% -> 9% of each run, Pallas kernels for 0% -> 0%
where the time goes in v5:
time: 132 us; the launch traced here: 131 us
  waiting for transfers between devices  64.6 us (49%)
  starting transfers between devices  22.2 us (17%)
  between operations  14.1 us (11%)
  Pallas kernels  12.9 us (10%)
  matrix products  11.1 us (8%)
  other arithmetic  3.81 us (3%)
  local copies, waits for them, and re-layouts  2.59 us (2%)
    all_to_all x1, waiting for transfers between devices, local(): pieces = lax.all_to_all(pieces, ('y', 'x'), 0, 0)  48.9 us
    all_to_all x1, starting transfers between devices, local(): stats = lax.all_to_all(stats, ('y', 'x'), 0, 0)  13 us
    pallas_call x1, Pallas kernels, front(): pl.pallas_call(front_kernel, name='front', out_shape=(jax.ShapeDtypeStruc...  9.68 us
    all_to_all x1, waiting for transfers between devices, local(): stats = lax.all_to_all(stats, ('y', 'x'), 0, 0)  8.8 us
    dot_general x1, matrix products, local(): head_term = jnp.dot(factor, both, preferred_element_type=jnp.float32)  5.79 us
    reduce_scatter x1, waiting for transfers between devices, local(): lax.psum_scatter(head_term.astype(jnp.bfloat16), 'z', scatter_dimension=0...  5.71 us
    all_to_all x1, starting transfers between devices, local(): pieces = lax.all_to_all(pieces, ('y', 'x'), 0, 0)  5.34 us
    dot_general x1, matrix products, local(): lax.dot_general(dlogits, weight_t, (((0,), (0,)), ((), ())), preferred_el...  5.32 us
  transfers between devices with their start and end apart: 5, of which 4 were waited for; matrix products, arithmetic and copies ran while one was open for 9% of the time, Pallas kernels for 0%

profile of v5, /device:TPU:2, one launch (start us, length us, event | category | flops | bytes accessed | tf_op | source)
XLA Modules:
  0.0 131.4 jit_solution(17647838907027458454)
XLA Ops:
  7.2 0.0 copy-start
  7.2 9.7 %front.1 = (bf16[128,8192]{1,0:T(8,128)(2,1)}, f32[128,1]{1,0:T(8,128)}, f32[528,128]{1,0:T(8,128)}, f32[528,128]{1,0:T(8,128)}, f32[32,4,128]{2,1,0:T(4,128)}) custom-call(s32[1]{0:T(128)} %bitcast.start_ref, bf16[128,8192]{1,0:T(8,128)(2,1)} %x_hbm.1, f32[1,8192]{1,0:T(1,128)} %bitcast.36, bf16[528,8192]{1,0:T(8,128)(2,1)} %bitcast.26, ...), custom_call_target="tpu_custom_call" | custom-call | flops 1107296256 | bytes 12845056 | tf_op jit(solution)/shard_map/front/pallas_call | solution.py:95
  16.9 1.9 %collective-permute-start.1 = (bf16[128,8192]{1,0:T(8,128)(2,1)}, bf16[128,8192]{1,0:T(8,128)(2,1)}, u32[]{:S(2)}, u32[]{:S(2)}) collective-permute-start(bf16[128,8192]{1,0:T(8,128)(2,1)} %get-tuple-element.12), channel_id=1, source_target_pairs={{0,32},{32,0},{1,33},{33,1},{2,34},{34,2},{3,35},{35,3},{4,36},{36... | collective-permute-start | bytes 6291464 | tf_op jit(solution)/shard_map/ppermute | solution.py:158
  18.8 13.0 %all-to-all-start = ((f32[32,4,128]{2,1,0:T(4,128)}), f32[32,4,128]{2,1,0:T(4,128)S(1)}, u32[]{:S(2)}, u32[]{:S(2)}) async-start(f32[32,4,128]{2,1,0:T(4,128)} %get-tuple-element.8), calls=%async_computation | async-start | bytes 131072 | tf_op jit(solution)/shard_map/all_to_all | solution.py:160
  31.8 0.0 reduce-scatter.2.cloned.1.call-start
  31.9 0.0 copy-done
  31.9 8.8 %all-to-all-done = f32[32,4,128]{2,1,0:T(4,128)S(1)} async-done(((f32[32,4,128]{2,1,0:T(4,128)}), f32[32,4,128]{2,1,0:T(4,128)S(1)}, u32[]{:S(2)}, u32[]{:S(2)}) %all-to-all-start) | async-done | bytes 65568 | tf_op jit(solution)/shard_map/all_to_all | solution.py:160
  40.7 0.1 fusion.11
  40.9 0.5 subtract_add_fusion
  41.4 1.1 subtract_convert_fusion
  42.6 1.9 %collective-permute-start = (bf16[288,128]{1,0:T(8,128)(2,1)S(1)}, bf16[288,128]{1,0:T(8,128)(2,1)S(1)}, u32[]{:S(2)}, u32[]{:S(2)}) collective-permute-start(bf16[288,128]{1,0:T(8,128)(2,1)S(1)} %bitcast.32), channel_id=1, source_target_pairs={{0,32},{32,0},{1,33},{33,1},{2,34},{34,2},{3,35},{35,3},{4,36},{36... | collective-permute-start | bytes 221192 | tf_op jit(solution)/shard_map/ppermute | solution.py:178
  44.5 1.2 collective-permute-done
  45.7 0.0 collective-permute-done.1
  45.7 5.8 %convolution_convert_fusion = bf16[288,8192]{1,0:T(8,128)(2,1)} fusion(bf16[128,8192]{1,0:T(8,128)(2,1)} %collective-permute-done.1, bf16[128,8192]{1,0:T(8,128)(2,1)} %get-tuple-element.12, bf16[288,128]{1,0:T(8,128)(2,1)S(1)} %collective-permute-done, bf16[288,128]{1,0:T(8,128)(2,1)S(1)} %bitcast.31), kind=kOutput, calls=%fused_computation | convolution fusion | flops 1219002368 | bytes 9060352 | tf_op jit(solution)/shard_map/dot_general | solution.py:188
  51.5 0.0 reduce-scatter.2.cloned.1.call-update
  51.5 5.3 %convolution_convert_fusion.1 = bf16[128,8192]{1,0:T(8,128)(2,1)S(1)} fusion(bf16[528,128]{1,0:T(8,128)(2,1)S(1)} %subtract_convert_fusion, bf16[8192,528]{0,1:T(8,128)(2,1)} %param.8), kind=kOutput, calls=%fused_computation.1 | convolution fusion | flops 1108344832 | bytes 10883072 | tf_op jit(solution)/shard_map/dot_general | solution.py:181
  56.9 0.0 copy-start.1
  56.9 1.6 %copy.23 = bf16[16,32,8,256]{3,2,0,1:T(8,128)(2,1)} copy(bf16[16,32,8,256]{3,2,1,0:T(8,128)(2,1)S(1)} %bitcast.27) | data formatting | bytes 4194304 | tf_op jit(solution)/shard_map/reshape | solution.py:184
  58.5 5.3 %all-to-all-start.1 = ((bf16[32,128,256]{2,1,0:T(8,128)(2,1)}), bf16[32,128,256]{2,1,0:T(8,128)(2,1)S(1)}, u32[]{:S(2)}, u32[]{:S(2)}) async-start(bf16[32,128,256]{2,1,0:T(8,128)(2,1)} %bitcast.28), calls=%async_computation.1 | async-start | bytes 4194304 | tf_op jit(solution)/shard_map/all_to_all | solution.py:185
  63.9 0.8 dynamic_slice.13
  64.6 0.1 copy.18
  64.7 0.0 copy-done.1
  64.7 0.1 fusion.10
  64.9 48.9 %all-to-all-done.1 = bf16[32,128,256]{2,1,0:T(8,128)(2,1)S(1)} async-done(((bf16[32,128,256]{2,1,0:T(8,128)(2,1)}), bf16[32,128,256]{2,1,0:T(8,128)(2,1)S(1)}, u32[]{:S(2)}, u32[]{:S(2)}) %all-to-all-start.1) | async-done | bytes 2097184 | tf_op jit(solution)/shard_map/all_to_all | solution.py:185
  113.8 0.3 convert_reduce_fusion
  114.0 1.6 %subtract_convert_fusion.1 = bf16[128,256]{1,0:T(8,128)(2,1)} fusion(f32[128,256]{1,0:T(8,128)S(1)} %convert_reduce_fusion, f32[128]{0:T(128)S(1)} %get-tuple-element.14, f32[128]{0:T(128)S(1)} %get-tuple-element.15, bf16[128,8192]{1,0:T(8,128)(2,1)} %x_hbm.1, s32[]{:T(128)S(6)} %select_n.11, f32[128]{0:T(128)S(1)} %get-tuple-element.13, ...), kind=kLoop, calls=%fused_computation.11 | loop fusion | flops 229376 | bytes 264708 | tf_op jit(solution)/shard_map/convert_element_type | solution.py:199
  115.6 5.7 %reduce-scatter.2.cloned.1.call-done.in_ref = bf16[24,8192]{1,0:T(8,128)(2,1)} async-done(((bf16[288,8192]{1,0:T(8,128)(2,1)}), bf16[24,8192]{1,0:T(8,128)(2,1)}) %reduce-scatter.2.cloned.1.call-update) | async-done | bytes 393232 | tf_op jit(solution)/shard_map/reduce_scatter | solution.py:189
  121.4 3.2 %spread.1 = f32[22,1,8192]{2,1,0:T(1,128)} custom-call(bf16[24,8192]{1,0:T(8,128)(2,1)} %reduce-scatter.2.cloned.1.call-done.in_ref), custom_call_target="tpu_custom_call" | custom-call | bytes 1441792 | tf_op jit(solution)/shard_map/spread/pallas_call | solution.py:133
  (6 shorter events, 0.2 us)
Async XLA Ops:
  7.2 24.7 %copy-start = (f32[128,16]{0,1:T(8,128)S(1)}, f32[128,16]{0,1:T(8,128)}, u32[]{:S(2)}) copy-start(f32[128,16]{0,1:T(8,128)} %param.10) | copy-start | bytes 24580
  16.9 28.8 %collective-permute-start.1 = (bf16[128,8192]{1,0:T(8,128)(2,1)}, bf16[128,8192]{1,0:T(8,128)(2,1)}, u32[]{:S(2)}, u32[]{:S(2)}) collective-permute-start(bf16[128,8192]{1,0:T(8,128)(2,1)} %get-tuple-element.12), channel_id=1, source_target_pairs={{0,32},{32,0},{1,33},{33,1},{2,34},{34,2},{3,35},{35,3},{4,36},{36... | collective-permute-start | bytes 6291464 | tf_op jit(solution)/shard_map/ppermute | solution.py:158
  18.8 21.9 %all-to-all-start = ((f32[32,4,128]{2,1,0:T(4,128)}), f32[32,4,128]{2,1,0:T(4,128)S(1)}, u32[]{:S(2)}, u32[]{:S(2)}) async-start(f32[32,4,128]{2,1,0:T(4,128)} %get-tuple-element.8), calls=%async_computation | async-start | bytes 131072 | tf_op jit(solution)/shard_map/all_to_all | solution.py:160
  31.8 89.5 %reduce-scatter.2.cloned.1.call-start = ((), (), s32[]{:S(2)}) async-start(), calls=%async_computation.3 | async-start | bytes 5111808 | tf_op jit(solution)/shard_map/reduce_scatter | solution.py:189
  42.6 3.2 %collective-permute-start = (bf16[288,128]{1,0:T(8,128)(2,1)S(1)}, bf16[288,128]{1,0:T(8,128)(2,1)S(1)}, u32[]{:S(2)}, u32[]{:S(2)}) collective-permute-start(bf16[288,128]{1,0:T(8,128)(2,1)S(1)} %bitcast.32), channel_id=1, source_target_pairs={{0,32},{32,0},{1,33},{33,1},{2,34},{34,2},{3,35},{35,3},{4,36},{36... | collective-permute-start | bytes 221192 | tf_op jit(solution)/shard_map/ppermute | solution.py:178
  56.9 7.9 %copy-start.1 = (f32[128,1]{1,0:T(8,128)S(1)}, f32[128,1]{1,0:T(8,128)}, u32[]{:S(2)}) copy-start(f32[128,1]{1,0:T(8,128)} %get-tuple-element.11) | copy-start | bytes 1540
  58.5 55.2 %all-to-all-start.1 = ((bf16[32,128,256]{2,1,0:T(8,128)(2,1)}), bf16[32,128,256]{2,1,0:T(8,128)(2,1)S(1)}, u32[]{:S(2)}, u32[]{:S(2)}) async-start(bf16[32,128,256]{2,1,0:T(8,128)(2,1)} %bitcast.28), calls=%async_computation.1 | async-start | bytes 4194304 | tf_op jit(solution)/shard_map/all_to_all | solution.py:185
Sparse Core Ops, SparseCore 0:
  51.7 69.6 reduce-scatter.1
